TPU v7x, 32 devices: a whole 2x2x4 slice. The times are simulated.
32 devices in a mesh: groups: 2 (over y), dp: 4 (over z), section: 4 (over x, core).
Axes of the slice: x: 2, y: 2, z: 4, core: 2. Of those that a mesh axis runs over, the one named last changes fastest.
Arguments:
- top_pair: bfloat16 [3072, 3072], P(('groups', 'dp')), parts along dimension 0, may hold values from -48 to 48
- kept: int32 [8], P('groups'), parts along dimension 0, may hold values from 128 to 384, as said below
- teacher: int32 [8], P('groups'), parts along dimension 0, may hold values from -1024 to 1023
- down_proj: bfloat16 [4, 2, 1536, 256], P('section', None, 'dp'), may hold values from -0.15625 to 0.15625
- up_proj: bfloat16 [4, 2, 256, 1536], P('section', None, 'dp'), may hold values from -0.375 to 0.375
- gains: bfloat16 [4, 2, 1536], P('section'), may hold values from 0.099609375 to 1.8984375
- head_proj: bfloat16 [3072, 128], P('dp'), may hold values from -0.109375 to 0.109375
- head_gain: bfloat16 [3072], replicated, may hold values from 0.099609375 to 1.8984375
- head_out: bfloat16 [128], replicated, may hold values from -0.5 to 0.5
Outputs:
- pair_grads: bfloat16 [4, 3072, 3072], P('section', ('groups', 'dp')), parts along dimension 1
- down_grad: float32 [8, 2, 1536, 256], P(('groups', 'section'), None, 'dp'), parts along dimension 0
- up_grad: float32 [8, 2, 256, 1536], P(('groups', 'section'), None, 'dp'), parts along dimension 0
- gain_grad: float32 [8, 2, 1536], P(('groups', 'section'), None, 'dp'), parts along dimension 0
There are 2 independent parts, one for each index of `groups`. A program takes and returns all parts, laid end to end along the dimension named above; an argument that names none is the same for every part. Nothing has to cross between parts.
Inputs may be any that keep to these rules, and one draw needn't show every extreme that they name: `kept`: in each aligned group of four passages (4i to 4i + 3) exactly one keeps 3 * 128 tokens and the other three keep 128.
All inputs are finite; a program needn't handle non-finite values.
Results may differ from a plain program's by a relative error of at most 0.03.
Values may be sent and summed in bfloat16 or wider, within the bound.
No kernel may reach another device: no remote copies, remote signals or barrier semaphores. Data moves between devices by JAX's collectives and lax.ppermute only.
A program may use at most 128 MiB of HBM per device.

v0:
```python
import functools

import jax
import jax.numpy as jnp
from jax import lax
from jax.experimental import pallas as pl
from jax.experimental.pallas import tpu as pltpu
from jax.sharding import PartitionSpec as P


EPS = 1e-06
LOSS_SCALE = 4096.0
FIXED_POINT = 256.0
QUAD = 4
LONG = 3
F32 = jnp.float32
BF16 = jnp.bfloat16
ANY = pl.BlockSpec(memory_space=pl.ANY)
HBM = pl.BlockSpec(memory_space=pltpu.HBM)
VMEM = pl.BlockSpec(memory_space=pltpu.VMEM)


def dot(left, right):
    return jnp.dot(left, right, preferred_element_type=F32)


def dot_nt(left, right):
    return lax.dot_general(left, right, (((1,), (1,)), ((), ())), preferred_element_type=F32)


def dot_tn(left, right):
    return lax.dot_general(left, right, (((0,), (0,)), ((), ())), preferred_element_type=F32)


def norm_parts(rows):
    values = rows.astype(F32)
    inverse = lax.rsqrt(jnp.mean(values * values, axis=-1, keepdims=True) + EPS)
    return values * inverse, inverse


def head_logits(normed, gain_ref, scaled_ref, meta_ref, pieces):
    scaled_ref[...] = (normed * gain_ref[...].astype(F32)).astype(BF16)
    part = pieces[0].shape[0]
    total = None
    for k, piece in enumerate(pieces):
        start = pl.multiple_of(meta_ref[0, 8 + k] * part, part)
        term = dot(scaled_ref[:, pl.ds(start, part)], piece[...])
        total = term if total is None else total + term
    return total


def score_kernel(count, unit, meta_ref, kept_ref, teacher_ref, rows_ref, gain_ref, out_ref, *rest):
    pieces, (coef_ref, scaled_ref) = rest[:count], rest[count:]
    step = pl.program_id(0)
    kept = kept_ref[meta_ref[0, 5]]

    @pl.when(step == 0)
    def _():
        coef_ref[...] = jnp.zeros_like(coef_ref)

    @pl.when(jnp.logical_and(meta_ref[0, 4] == 1, step * unit < kept))
    def _():
        normed, _ = norm_parts(rows_ref[...])
        logits = head_logits(normed, gain_ref, scaled_ref, meta_ref, pieces)
        scores = jax.nn.silu(logits) * out_ref[...].astype(F32)
        place = lax.broadcasted_iota(jnp.int32, scores.shape, 0) + step * unit
        scores = jnp.where(place < kept, scores, 0.0)
        coef_ref[...] += jnp.broadcast_to(jnp.sum(scores), coef_ref.shape)

    @pl.when(step == pl.num_programs(0) - 1)
    def _():
        counts = jnp.full(coef_ref.shape, kept, jnp.int32).astype(F32)
        target = jnp.full(coef_ref.shape, teacher_ref[meta_ref[0, 5]], jnp.int32).astype(F32)
        score = coef_ref[...] / counts
        coef_ref[...] = 2.0 * LOSS_SCALE * (score - target / FIXED_POINT) / counts


def score_call(meta, kept, teacher, rows, gain, out, pieces, unit):
    slots, width = rows.shape
    keep = lambda *_: (0, 0)
    return pl.pallas_call(
        functools.partial(score_kernel, len(pieces), unit),
        grid_spec=pltpu.PrefetchScalarGridSpec(
            num_scalar_prefetch=3,
            grid=(slots // unit,),
            in_specs=[
                pl.BlockSpec((unit, width), lambda i, *_: (i, 0)),
                pl.BlockSpec(gain.shape, keep),
                pl.BlockSpec(out.shape, keep),
            ]
            + [pl.BlockSpec(p.shape, keep) for p in pieces],
            out_specs=pl.BlockSpec((8, 128), keep),
            scratch_shapes=[pltpu.VMEM((unit, width), BF16)],
        ),
        out_shape=jax.ShapeDtypeStruct((8, 128), F32),
        cost_estimate=pl.CostEstimate(
            flops=2 * slots * width * out.shape[1],
            transcendentals=slots * out.shape[1],
            bytes_accessed=12 * slots * width,
        ),
        compiler_params=pltpu.CompilerParams(vmem_limit_bytes=24 << 20),
        name="score",
    )(meta, kept, teacher, rows, gain, out, *pieces)


def head_kernel(count, meta_ref, dealt_ref, rows_ref, far_ref, own_ref, gain_ref, out_ref, *rest):
    pieces, (packet_ref, scaled_ref, normal_ref) = rest[:count], rest[count:]
    step = pl.program_id(0)

    @pl.when(meta_ref[0, 4] == 1)
    def _():
        rows = jnp.where(step == 0, dealt_ref[...], rows_ref[...])
        width = rows.shape[1]
        packet_ref[:, :width] = rows
        normed, inverse = norm_parts(rows)
        normal_ref[...] = normed
        logits = head_logits(normed, gain_ref, scaled_ref, meta_ref, pieces)
        coef = jnp.where(step == 0, far_ref[0:1, :], own_ref[0:1, :])
        sigma = jax.nn.sigmoid(logits)
        slope = sigma * (1.0 + logits * (1.0 - sigma))
        grad = (coef * out_ref[...].astype(F32) * slope).astype(BF16)
        part = pieces[0].shape[0]
        mean = jnp.zeros_like(inverse)
        spans = []
        for k, piece in enumerate(pieces):
            start = pl.multiple_of(meta_ref[0, 8 + k] * part, part)
            span = pl.ds(start, part)
            weighted = dot_nt(grad, piece[...]) * gain_ref[:, span].astype(F32)
            mean += jnp.sum(normal_ref[:, span] * weighted, axis=-1, keepdims=True)
            spans.append((span, weighted))
        mean = mean / normed.shape[1]
        for k, (span, weighted) in enumerate(spans):
            start = pl.multiple_of(meta_ref[0, 8 + k] * part + width, part)
            back = inverse * (weighted - normal_ref[:, span] * mean)
            packet_ref[:, pl.ds(start, part)] = back.astype(BF16)


def head_call(meta, dealt, rows, far, own, gain, out, pieces, total):
    block, width = dealt.shape
    keep = lambda *_: (0, 0)
    return pl.pallas_call(
        functools.partial(head_kernel, len(pieces)),
        grid_spec=pltpu.PrefetchScalarGridSpec(
            num_scalar_prefetch=1,
            grid=(total // block,),
            in_specs=[
                pl.BlockSpec((block, width), keep),
                pl.BlockSpec((block, width), lambda i, *_: (jnp.maximum(i - 1, 0), 0)),
                pl.BlockSpec((8, 128), keep),
                pl.BlockSpec((8, 128), keep),
                pl.BlockSpec(gain.shape, keep),
                pl.BlockSpec(out.shape, keep),
            ]
            + [pl.BlockSpec(p.shape, keep) for p in pieces],
            out_specs=pl.BlockSpec((block, 2 * width), lambda i, *_: (i, 0)),
            scratch_shapes=[pltpu.VMEM((block, width), BF16), pltpu.VMEM((block, width), F32)],
        ),
        out_shape=jax.ShapeDtypeStruct((total, 2 * width), BF16),
        cost_estimate=pl.CostEstimate(
            flops=4 * total * width * out.shape[1],
            transcendentals=total * out.shape[1],
            bytes_accessed=24 * total * width,
        ),
        compiler_params=pltpu.CompilerParams(vmem_limit_bytes=24 << 20),
        name="head",
    )(meta, dealt, rows, far, own, gain, out, *pieces)


def pack_kernel(deals, meta_ref, down_ref, up_ref, rows_ref, *refs):
    outs, (message_s, deal_s, sem) = refs[: 2 + deals], refs[2 + deals :]
    count, rank = outs[0].shape[0] // 2, outs[0].shape[2]
    copies = []

    def copy(source, goal):
        copies.append(pltpu.make_async_copy(source, goal, sem.at[len(copies)]))
        copies[-1].start()

    for number, field in enumerate((3, 6)):
        index = meta_ref[0, field]
        copy(down_ref.at[index], message_s.at[number, pl.ds(0, count)])
        for c in range(count):
            copy(up_ref.at[index, :, pl.ds(c * rank, rank)], message_s.at[number, count + c])
    for k in range(deals):
        rows = deal_s.shape[1]
        start = pl.multiple_of(meta_ref[0, 20 + k], rows)
        copy(rows_ref.at[pl.ds(start, rows)], deal_s.at[k])
    each = 1 + count
    for number in range(2):
        for one in copies[number * each : (number + 1) * each]:
            one.wait()
        copy(message_s.at[number], outs[number])
    for k in range(deals):
        copies[2 * each + k].wait()
        copy(deal_s.at[k], outs[2 + k])
    for one in copies[2 * each + deals :]:
        one.wait()


def pack_call(meta, down, up, rows, deals, chunk):
    part, half = up.shape[1:]
    rank = down.shape[2]
    count = half // rank
    message = jax.ShapeDtypeStruct((2 * count, part, rank), BF16)
    deal = jax.ShapeDtypeStruct((chunk, rows.shape[1]), BF16)
    return pl.pallas_call(
        functools.partial(pack_kernel, deals),
        grid_spec=pltpu.PrefetchScalarGridSpec(
            num_scalar_prefetch=1,
            grid=(1,),
            in_specs=[HBM] * 3,
            out_specs=[HBM] * (2 + deals),
            scratch_shapes=[
                pltpu.VMEM((2,) + message.shape, BF16),
                pltpu.VMEM((deals,) + deal.shape, BF16),
                pltpu.SemaphoreType.DMA((2 * (2 + count) + 2 * deals,)),
            ],
        ),
        out_shape=[message] * 2 + [deal] * deals,
        compiler_params=pltpu.CompilerParams(vmem_limit_bytes=60 << 20),
        name="pack",
    )(meta, down.reshape(2, count, part, rank), up, rows)


def assemble_kernel(plan, meta_ref, *refs):
    pieces, (down_ref, up_ref, sem) = refs[: len(plan)], refs[len(plan) :]
    spans = up_ref.shape[1]

    def each(action):
        for number, (ref, (branch_field, place_field, valid_field)) in enumerate(zip(pieces, plan)):
            index, spot = meta_ref[0, branch_field], meta_ref[0, place_field]
            part = ref.shape[1]
            start = pl.multiple_of(spot * part, part)
            copies = [
                pltpu.make_async_copy(
                    ref.at[pl.ds(0, spans)],
                    down_ref.at[index, pl.ds(spot * spans, spans)],
                    sem.at[2 * number],
                ),
                pltpu.make_async_copy(
                    ref.at[pl.ds(spans, spans)],
                    up_ref.at[index, :, pl.ds(start, part)],
                    sem.at[2 * number + 1],
                ),
            ]

            @pl.when(meta_ref[0, valid_field] == 1)
            def _():
                for copy in copies:
                    action(copy)

    each(lambda copy: copy.start())
    each(lambda copy: copy.wait())


def assemble_call(meta, pieces, plan, half):
    rank = pieces[0].shape[2]
    part = pieces[0].shape[1]
    return pl.pallas_call(
        functools.partial(assemble_kernel, plan),
        grid_spec=pltpu.PrefetchScalarGridSpec(
            num_scalar_prefetch=1,
            grid=(1,),
            in_specs=[ANY] * len(pieces),
            out_specs=[VMEM] * 2,
            scratch_shapes=[pltpu.SemaphoreType.DMA((2 * len(pieces),))],
        ),
        out_shape=[
            jax.ShapeDtypeStruct((2, half // part, part, rank), BF16),
            jax.ShapeDtypeStruct((2, half // rank, rank, rank), BF16),
        ],
        compiler_params=pltpu.CompilerParams(vmem_limit_bytes=8 << 20),
        name="assemble",
    )(meta, *pieces)


def output_kernel(unit, meta_ref, kept_ref, pairs_ref, *refs):
    pieces, (out_ref, zero_s, sem) = refs[:QUAD], refs[QUAD:]
    chunk = pieces[0].shape[0]
    own = pltpu.make_async_copy(
        pairs_ref.at[pl.ds(chunk, unit)], out_ref.at[pl.ds(0, unit)], sem.at[QUAD]
    )
    own.start()
    long = kept_ref[meta_ref[0, 5]] > unit
    zero_s[...] = jnp.zeros_like(zero_s)
    for k, piece in enumerate(pieces):
        start = pl.multiple_of(meta_ref[0, 23 + k], chunk)
        goal = out_ref.at[pl.ds(start, chunk)]

        @pl.when(long)
        def _():
            pltpu.make_async_copy(piece, goal, sem.at[k]).start()

        @pl.when(jnp.logical_not(long))
        def _():
            pltpu.make_async_copy(zero_s, goal, sem.at[k]).start()

    for k in range(QUAD):
        start = pl.multiple_of(meta_ref[0, 23 + k], chunk)
        pltpu.make_async_copy(zero_s, out_ref.at[pl.ds(start, chunk)], sem.at[k]).wait()
    own.wait()


def output_call(meta, kept, pairs, pieces, slots):
    chunk, width = pieces[0].shape
    return pl.pallas_call(
        functools.partial(output_kernel, slots // LONG),
        grid_spec=pltpu.PrefetchScalarGridSpec(
            num_scalar_prefetch=2,
            grid=(1,),
            in_specs=[ANY] * (1 + len(pieces)),
            out_specs=ANY,
            scratch_shapes=[
                pltpu.VMEM((chunk, width), BF16),
                pltpu.SemaphoreType.DMA((QUAD + 1,)),
            ],
        ),
        out_shape=jax.ShapeDtypeStruct((slots, width), BF16),
        compiler_params=pltpu.CompilerParams(vmem_limit_bytes=4 << 20),
        name="output",
    )(meta, kept, pairs, *pieces)


def stage_kernel(slot, held, firsts, *refs):
    meta_ref, gain_ref, top_ref, down_s, up_s = refs[:5]
    arrived = dict(zip(held, refs[5 : 5 + len(held)]))
    rest = refs[5 + len(held) + (3 + firsts if slot else 0) :]
    packet_ref, pairs_ref, saved_ref, sums_ref = rest[:4]
    first_ref = rest[4] if firsts else None
    packet_s, packet_sem = rest[4 + firsts :]
    rows, wide = packet_s.shape
    width = wide // 2
    half = width // 2
    spans, rank = up_s.shape[1], up_s.shape[2]
    per = down_s.shape[1] // spans
    source, micro = meta_ref[slot, 0], meta_ref[slot, 1]

    @pl.when(meta_ref[slot, 2] == 1)
    def _():
        place = pl.ds(pl.multiple_of(micro * rows, rows), rows)
        options = [
            (
                source == 0,
                [pltpu.make_async_copy(top_ref.at[place], packet_s, packet_sem.at[0])],
            )
        ]
        for kind, ref in arrived.items():
            copy = pltpu.make_async_copy(ref, packet_s, packet_sem.at[1 + kind])
            options.append((source == kind, [copy]))

        def each_option(action):
            for chosen, copies in options:

                @pl.when(chosen)
                def _():
                    for copy in copies:
                        action(copy)

        each_option(lambda copy: copy.start())
        each_option(lambda copy: copy.wait())

        def branch(index, values_ref, start, cot, base, less, goal, plus, result):
            def span(c):
                return slice(c * rank, (c + 1) * rank)

            def take(ref, origin, c):
                return ref[:, origin + c * rank : origin + (c + 1) * rank].astype(F32)

            total = None
            for c in range(spans):
                values = take(values_ref, start, c)
                term = jnp.sum(values * values, axis=-1, keepdims=True)
                total = term if total is None else total + term
            inverse = lax.rsqrt(total / half + EPS)
            for c in range(spans):
                gain = gain_ref[index : index + 1, span(c)].astype(F32)
                scaled = (take(values_ref, start, c) * inverse * gain).astype(BF16)
                saved_ref[place, base + c * rank : base + (c + 1) * rank] = scaled
            down = down_s[index].reshape(half, rank)
            pre = dot(saved_ref[place, base : base + half], down)
            sigma = jax.nn.sigmoid(pre)
            hidden = (pre * sigma).astype(BF16)
            saved_ref[place, base + half : base + half + rank] = hidden
            grad_hidden = None
            for c in range(spans):
                term = dot_nt(cot(c), up_s[index, c])
                grad_hidden = term if grad_hidden is None else grad_hidden + term
            slope = sigma * (1.0 + pre * (1.0 - sigma))
            grad_pre = (grad_hidden * slope).astype(BF16)
            saved_ref[place, base + half + rank : base + half + 2 * rank] = grad_pre
            mean = jnp.sum(grad_pre.astype(F32) * pre, axis=-1, keepdims=True) / half
            for c in range(spans):
                output = dot(hidden, up_s[index, c])
                packet_ref[:, goal + c * rank : goal + (c + 1) * rank] = (
                    take(packet_s, less, c) - output
                ).astype(BF16)
            for c in range(spans):
                part = down_s[index, c * per : (c + 1) * per].reshape(rank, rank)
                grad_scaled = dot_nt(grad_pre, part)
                normed = take(values_ref, start, c) * inverse
                sums_ref[micro, index : index + 1, span(c)] = jnp.sum(
                    grad_scaled * normed, axis=0, keepdims=True
                )
                gain = gain_ref[index : index + 1, span(c)].astype(F32)
                back = inverse * (grad_scaled * gain - normed * mean)
                value = (take(packet_s, plus, c) + back).astype(BF16)
                packet_ref[:, result + c * rank : result + (c + 1) * rank] = value
                low = result - width + c * rank
                pairs_ref[place, low : low + rank] = value

        block = half + 2 * rank
        saved_ref[place, 2 * block :] = packet_s[:, width + half :]
        branch(
            1,
            packet_s,
            0,
            lambda c: packet_s[:, width + half + c * rank : width + half + (c + 1) * rank],
            block,
            half,
            half,
            width,
            width,
        )
        branch(
            0,
            packet_ref,
            half,
            lambda c: packet_ref[:, width + c * rank : width + (c + 1) * rank],
            0,
            0,
            0,
            width + half,
            width + half,
        )
        if firsts:

            @pl.when(micro == 0)
            def _():
                first_ref[...] = packet_ref[:, width:]


def stage_call(slot, meta, gains, top, weights, arrived, state, shapes):
    _, wide = top.shape
    half, rank = wide // 4, weights[0].shape[3]
    rows = shapes[-1].shape[0]
    held = tuple(arrived)
    n_in = 5 + len(held)
    shapes = shapes[: len(state)] if slot else shapes
    packet, *state = pl.pallas_call(
        functools.partial(stage_kernel, slot, held, len(shapes) - 3),
        grid_spec=pltpu.PrefetchScalarGridSpec(
            num_scalar_prefetch=1,
            grid=(1,),
            in_specs=[pl.BlockSpec(gains.shape, lambda *_: (0, 0)), ANY]
            + [VMEM] * (2 + len(held) + len(state)),
            out_specs=[VMEM] * (1 + len(shapes)),
            scratch_shapes=[pltpu.VMEM((rows, wide), BF16), pltpu.SemaphoreType.DMA((4,))],
        ),
        out_shape=[jax.ShapeDtypeStruct((rows, wide), BF16)] + shapes,
        input_output_aliases={n_in + i: 1 + i for i in range(len(state))},
        cost_estimate=pl.CostEstimate(
            flops=16 * 2 * rows * half * rank, transcendentals=0, bytes_accessed=4 * rows * wide
        ),
        compiler_params=pltpu.CompilerParams(vmem_limit_bytes=6 << 20),
        name="stage",
    )(meta, gains, top, *weights, *arrived.values(), *state)
    return packet, state


def weight_kernel(fields, meta_ref, saved_ref, first_ref, sums_ref, *refs):
    outs = refs[: len(fields)]
    down_s, up_s, gain_s, sem = refs[len(fields) :]
    spans, rank = up_s.shape[1], up_s.shape[2]
    half = spans * rank
    part = outs[0].shape[1]
    parts = rank // part
    block = half + 2 * rank
    copies = []

    def send(source, goal):
        copies.append(pltpu.make_async_copy(source, goal, sem.at[len(copies)]))
        copies[-1].start()

    spots = [meta_ref[0, field] for field in fields]
    for index in (1, 0):
        base = block * index
        scaled = saved_ref[:, base : base + half]
        hidden = saved_ref[:, base + half : base + half + rank]
        grad_pre = saved_ref[:, base + half + rank : base + block]
        cot = saved_ref[:, 2 * block : 2 * block + half] if index == 1 else first_ref[:, :half]
        for c in range(spans):
            up_s[index, c] = dot_tn(hidden, cot[:, c * rank : (c + 1) * rank]).astype(BF16)
        for out, spot in zip(outs, spots):
            start = pl.multiple_of(spot * part, part)
            send(
                up_s.at[index, :, pl.ds(start, part)],
                out.at[pl.ds((2 * index + 1) * spans, spans)],
            )
        down_s[index] = dot_tn(scaled, grad_pre).astype(BF16).reshape(down_s.shape[1:])
        for out, spot in zip(outs, spots):
            send(
                down_s.at[index, pl.ds(spot * spans, spans)],
                out.at[pl.ds(2 * index * spans, spans)],
            )
    gain_s[...] = jnp.zeros_like(gain_s)
    for number, (out, spot) in enumerate(zip(outs, spots)):
        size = half // parts
        for row, low in enumerate(range(0, size, rank)):
            high = min(low + rank, size)
            start = pl.multiple_of(spot * size + low, 128)
            gain = jnp.sum(sums_ref[:, :, pl.ds(start, high - low)], axis=0)
            gain_s[number, 0, 8 * row : 8 * row + 8, 0 : high - low] = gain.astype(BF16)
        send(gain_s.at[number], out.at[pl.ds(4 * spans, 1)])
    for copy in copies:
        copy.wait()


def weight_call(meta, saved, pairs, sums, fields, parts, half, rank):
    spans, part = half // rank, rank // parts
    return pl.pallas_call(
        functools.partial(weight_kernel, fields),
        grid_spec=pltpu.PrefetchScalarGridSpec(
            num_scalar_prefetch=1,
            grid=(1,),
            in_specs=[VMEM] * 3,
            out_specs=[HBM] * len(fields),
            scratch_shapes=[
                pltpu.VMEM((2, parts * spans, part, rank), BF16),
                pltpu.VMEM((2, spans, rank, rank), BF16),
                pltpu.VMEM((len(fields), 1, part, rank), BF16),
                pltpu.SemaphoreType.DMA((5 * len(fields),)),
            ],
        ),
        out_shape=[jax.ShapeDtypeStruct((4 * spans + 1, part, rank), BF16)] * len(fields),
        compiler_params=pltpu.CompilerParams(vmem_limit_bytes=16 << 20),
        name="weight",
    )(meta, saved, pairs, sums)


def total_kernel(count, scale, *refs):
    messages, (down_ref, up_ref, gain_ref) = refs[:count], refs[count:]
    spans = up_ref.shape[2] // messages[0].shape[2]
    rank = messages[0].shape[2]

    def total(*where):
        out = messages[0][where].astype(F32)
        for message in messages[1:]:
            out += message[where].astype(F32)
        return out * scale

    for index in range(2):
        base = 2 * index * spans
        down_ref[index] = total(slice(base, base + spans))
        for c in range(spans):
            up_ref[index, :, c * rank : (c + 1) * rank] = total(base + spans + c)
    size = gain_ref.shape[1]
    for row, low in enumerate(range(0, size, rank)):
        high = min(low + rank, size)
        block = total(4 * spans)
        gain_ref[:, low:high] = block[8 * row : 8 * row + 2, 0 : high - low]


def total_call(messages, scale, half):
    _, part, rank = messages[0].shape
    spans = half // rank
    down, up, gain = pl.pallas_call(
        functools.partial(total_kernel, len(messages), scale),
        out_shape=[
            jax.ShapeDtypeStruct((2, spans, part, rank), F32),
            jax.ShapeDtypeStruct((2, part, half), F32),
            jax.ShapeDtypeStruct((2, spans * part), F32),
        ],
        compiler_params=pltpu.CompilerParams(vmem_limit_bytes=24 << 20),
        name="total",
    )(*messages)
    return down.reshape(2, spans * part, rank), up, gain


def device_program(top_pair, kept, teacher, down_proj, up_proj, gains, head_proj, head_gain, head_out):
    devices = lax.axis_size("dp")
    sections = lax.axis_size("section")
    own = lax.axis_index("dp")
    section = lax.axis_index("section")
    side = lax.axis_index("groups")
    slots, width = top_pair.shape
    half, rank = width // 2, down_proj.shape[3]
    unit = slots // LONG
    chunk = (LONG - 1) * unit // QUAD
    rows_total = unit + chunk
    micros = rows_total // chunk
    quads = devices // QUAD
    place = own % QUAD
    top = sections - 1
    via = 1 if sections == 4 else top
    direct = devices == QUAD and lax.axis_size("groups") == 2 and sections == 4
    parts = QUAD if direct else 1

    def shift_pairs(k, lane=None):
        out = []
        for q in range(quads):
            for i in range(QUAD):
                source, goal = QUAD * q + i, QUAD * q + (i + k) % QUAD
                if lane is not None:
                    source, goal = source * sections + lane, goal * sections + lane
                out.append((source, goal))
        return out

    ids = jnp.arange(devices, dtype=jnp.int32)
    is_longest = jnp.logical_and(ids // QUAD == own // QUAD, kept > unit)
    longest = jnp.sum(jnp.where(is_longest, ids % QUAD, 0))
    mine = 1 - side if direct else jnp.zeros((), jnp.int32)
    is_top = section == top

    offsets = {top: 0}
    for s in range(top, 0, -1):
        offsets[s - 1] = offsets[s] + (1 if s % 2 == 1 else 2)
    count = micros + offsets[0]
    behind = (top - section) + (top // 2 - section // 2)
    source = jnp.where(is_top, 0, jnp.where(section % 2 == 0, 1, 2))
    step = jnp.arange(count, dtype=jnp.int32) - behind
    last = parts - 1
    fields = [
        source,
        jnp.clip(step, 0, micros - 1),
        jnp.logical_and(step >= 0, step < micros),
        mine,
        is_top,
        own,
        1 - mine,
        own if direct else 0,
    ]
    fields += [(own - k) % parts for k in range(QUAD)]
    fields += [
        jnp.clip(own - 1, 0, last),
        jnp.clip(own + 1, 0, last),
        (own + 2) % parts,
        jnp.clip(last - own, 0, last),
        own >= 1,
        own <= 2,
        jnp.logical_or(own == 0, own == 3),
        1,
    ]
    fields += [unit + chunk * ((place + k) % QUAD) for k in range(1, QUAD)]
    fields += [unit + chunk * ((place - k) % QUAD) for k in range(QUAD)]
    meta = jnp.stack(
        [jnp.broadcast_to(jnp.asarray(f).astype(jnp.int32), (count,)) for f in fields], axis=1
    )

    if direct:
        down, up = down_proj[0], up_proj[0]
    else:
        down = lax.all_gather(down_proj[0], "dp", axis=1, tiled=True)
        up = lax.all_gather(up_proj[0], "dp", axis=1, tiled=True)
    mine_msg, other_msg, *deals = pack_call(meta, down, up, top_pair, QUAD - 1, chunk)
    pieces, plan = [mine_msg, other_msg], [(3, 7, 19), (6, 7, 19)]

    dealt = lax.dynamic_slice_in_dim(top_pair, unit + chunk * place, chunk)
    for k, deal in enumerate(deals, 1):
        other = lax.ppermute(deal, ("dp", "section"), shift_pairs(k, via))
        dealt = jnp.where((place - k) % QUAD == longest, other, dealt)
    if direct:
        head_pieces = [head_proj]
        for k in range(1, QUAD):
            piece = lax.ppermute(head_proj, ("dp", "section"), shift_pairs(k, via))
            head_pieces.append(lax.ppermute(piece, "section", [(via, top)]))
        dealt = lax.ppermute(dealt, "section", [(via, top)])

        def along(array, pairs):
            return lax.ppermute(array, "dp", pairs)

        def across(array, valid):
            pairs = [(QUAD * g + i, QUAD * (1 - g) + i) for g in (0, 1) for i in valid]
            return lax.ppermute(array, ("groups", "dp"), pairs)

        right = along(mine_msg, [(0, 1), (1, 2), (2, 3)])
        left = along(mine_msg, [(1, 0), (2, 1), (3, 2)])
        far = along(mine_msg, [(0, 2), (1, 3), (2, 0), (3, 1)])
        relay = along(far, [(1, 0), (2, 3)])
        gain_row, out_row = head_gain[None], head_out[None]
        coef = score_call(meta, kept, teacher, top_pair, gain_row, out_row, head_pieces, unit)
        relay, coef = lax.optimization_barrier((relay, coef))
        for piece, place_field, valid_field, valid in (
            (right, 12, 16, (1, 2, 3)),
            (left, 13, 17, (0, 1, 2)),
            (far, 14, 19, (0, 1, 2, 3)),
            (relay, 15, 18, (0, 3)),
        ):
            pieces += [piece, across(piece, valid)]
            plan += [(3, place_field, valid_field), (6, place_field, valid_field)]
    else:
        head_pieces = [lax.all_gather(head_proj, "dp", axis=0, tiled=True)]

    if not direct:
        gain_row, out_row = head_gain[None], head_out[None]
        coef = score_call(meta, kept, teacher, top_pair, gain_row, out_row, head_pieces, unit)
    far_coef = coef
    for k in range(1, QUAD):
        other = lax.ppermute(coef, ("dp", "section"), shift_pairs(k, top))
        far_coef = jnp.where((place - k) % QUAD == longest, other, far_coef)
    packets = head_call(meta, dealt, top_pair, far_coef, coef, gain_row, out_row, head_pieces, rows_total)

    shapes = [
        jax.ShapeDtypeStruct((rows_total, width), BF16),
        jax.ShapeDtypeStruct((rows_total, 2 * (half + 2 * rank) + half), BF16),
        jax.ShapeDtypeStruct((micros, 8, half), F32),
        jax.ShapeDtypeStruct((chunk, width), BF16),
    ]
    state = []
    weights = assemble_call(meta, pieces, plan, half)
    near, far_in = {}, {}
    for slot in range(count):
        arrived = {1: near.get(slot - 1), 2: far_in.get(slot - 2)}
        arrived = {kind: array for kind, array in arrived.items() if array is not None}
        packet, state = stage_call(slot, meta, gains[0], packets, weights, arrived, state, shapes)
        live = [s for s in range(1, sections) if 0 <= slot - offsets[s] < micros]
        for table, odd in ((near, 1), (far_in, 0)):
            hops = [(s, s - 1) for s in live if s % 2 == odd]
            if hops:
                table[slot] = lax.ppermute(packet, "section", hops)
        if slot == offsets[0]:
            piece = state.pop()
    pairs, saved, sums = state

    returned = [piece] + [lax.ppermute(piece, "dp", shift_pairs(k)) for k in range(1, QUAD)]
    grads_out = output_call(meta, kept, pairs, returned, slots)

    if direct:
        own_w, right_w, left_w, far_w, relay_w = weight_call(
            meta, saved, pairs, sums, (7, 13, 12, 14, 15), parts, half, rank
        )
        handed = along(relay_w, [(0, 1), (3, 2)])
        from_left = along(right_w, [(0, 1), (1, 2), (2, 3)])
        from_right = along(left_w, [(1, 0), (2, 1), (3, 2)])
        far_w = (far_w.astype(F32) + handed.astype(F32)).astype(BF16)
        from_far = along(far_w, [(0, 2), (1, 3), (2, 0), (3, 1)])
        messages = [own_w, from_left, from_right, from_far]
        down_sum, up_sum, gain_sum = total_call(messages, 1.0 / devices, half)
    else:
        (whole,) = weight_call(meta, saved, pairs, sums, (7,), parts, half, rank)
        down_sum, up_sum, gain_sum = total_call([whole], 1.0 / devices, half)
        scatter = functools.partial(lax.psum_scatter, axis_name="dp", scatter_dimension=1, tiled=True)
        down_sum, up_sum, gain_sum = scatter(down_sum), scatter(up_sum), scatter(gain_sum)
    return grads_out[None], down_sum[None], up_sum[None], gain_sum[None]


def solution(mesh):
    in_specs = (
        P(("groups", "dp"), None),
        P("groups"),
        P("groups"),
        P("section", None, "dp", None),
        P("section", None, "dp", None),
        P("section", None, None),
        P("dp", None),
        P(),
        P(),
    )
    out_specs = (
        P("section", ("groups", "dp"), None),
        P(("groups", "section"), None, "dp", None),
        P(("groups", "section"), None, "dp", None),
        P(("groups", "section"), None, "dp"),
    )
    return jax.shard_map(device_program, mesh=mesh, in_specs=in_specs, out_specs=out_specs, check_vma=False)
```

profile of v0, /device:TPU:0, one launch (start us, length us, event | category | flops | bytes accessed | tf_op | source)
XLA Modules:
  0.0 243.4 jit_solution(4288856647778812591)
XLA Ops:
  4.0 3.4 %pack.1 = (bf16[12,64,256]{2,1,0:T(8,128)(2,1)}, bf16[12,64,256]{2,1,0:T(8,128)(2,1)}, bf16[64,3072]{1,0:T(8,128)(2,1)}, bf16[64,3072]{1,0:T(8,128)(2,1)}, bf16[64,3072]{1,0:T(8,128)(2,1)}) custom-call(s32[7,27]{1,0:T(8,128)} %stack.2.meta_ref.refs_0_, bf16[2,6,64,256]{3,2,1,0:T(8,128)(2,1)} %bitcast.18, bf16[2,64,1536]{2,1,0:T(8,128)(2,1)} %bitcast.19, ...), custom_call_target="tpu_custom_call" | custom-call | tf_op jit(solution)/shard_map/pack/pallas_call | solution.py:205
  7.5 1.5 collective-permute-start
  9.0 1.4 collective-permute-start.1
  10.4 1.4 collective-permute-start.2
  12.5 4.1 %collective-permute-start.4 = (bf16[12,64,256]{2,1,0:T(8,128)(2,1)}, bf16[12,64,256]{2,1,0:T(8,128)(2,1)S(1)}, u32[]{:S(2)}, u32[]{:S(2)}) collective-permute-start(bf16[12,64,256]{2,1,0:T(8,128)(2,1)} %get-tuple-element.56.refs_0_), channel_id=1, source_target_pairs={{0,8},{4,12},{8,0},{12,4},{1,9},{5,13},{9,1},{13,5},{2,10},{6,14},... | collective-permute-start | bytes 1179656 | tf_op jit(solution)/shard_map/ppermute | solution.py:668
  19.9 1.3 collective-permute-start.17
  21.3 4.6 %collective-permute-start.15 = (bf16[12,64,256]{2,1,0:T(8,128)(2,1)}, bf16[12,64,256]{2,1,0:T(8,128)(2,1)S(1)}, u32[]{:S(2)}, u32[]{:S(2)}) collective-permute-start(bf16[12,64,256]{2,1,0:T(8,128)(2,1)} %get-tuple-element.56.refs_0_), channel_id=1, source_target_pairs={{0,4},{4,8},{8,12},{1,5},{5,9},{9,13},{2,6},{6,10},{10,14},{3,7},{... | collective-permute-start | bytes 1179656 | tf_op jit(solution)/shard_map/ppermute | solution.py:668
  27.2 2.3 collective-permute-done.4.refs_6_
  32.5 25.3 %collective-permute-done.5.refs_8_ = bf16[12,64,256]{2,1,0:T(8,128)(2,1)S(1)} collective-permute-done((bf16[12,64,256]{2,1,0:T(8,128)(2,1)S(1)}, bf16[12,64,256]{2,1,0:T(8,128)(2,1)S(1)}, u32[]{:S(2)}, u32[]{:S(2)}) %collective-permute-start.5) | collective-permute-done | bytes 393248 | tf_op jit(solution)/shard_map/ppermute | solution.py:668
  59.8 1.6 collective-permute-start.19
  61.4 2.4 collective-permute-start.18
  64.5 3.4 %collective-permute-start.20 = (bf16[12,64,256]{2,1,0:T(8,128)(2,1)S(1)}, bf16[12,64,256]{2,1,0:T(8,128)(2,1)S(1)}, u32[]{:S(2)}, u32[]{:S(2)}) collective-permute-start(bf16[12,64,256]{2,1,0:T(8,128)(2,1)S(1)} %collective-permute-done.5.refs_8_), channel_id=1, source_target_pairs={{0,16},{12,28},{16,0},{28,12},{1,17},{13,29},{17,1},{29,13},{2,18}... | collective-permute-start | bytes 1179656 | tf_op jit(solution)/shard_map/ppermute | solution.py:672
  68.7 5.2 %collective-permute-done.18.refs_5_ = bf16[12,64,256]{2,1,0:T(8,128)(2,1)S(1)} collective-permute-done((bf16[12,64,256]{2,1,0:T(8,128)(2,1)S(1)}, bf16[12,64,256]{2,1,0:T(8,128)(2,1)S(1)}, u32[]{:S(2)}, u32[]{:S(2)}) %collective-permute-start.18) | collective-permute-done | bytes 393248 | tf_op jit(solution)/shard_map/ppermute | solution.py:672
  73.9 8.4 %collective-permute-done.20.refs_9_ = bf16[12,64,256]{2,1,0:T(8,128)(2,1)S(1)} collective-permute-done((bf16[12,64,256]{2,1,0:T(8,128)(2,1)S(1)}, bf16[12,64,256]{2,1,0:T(8,128)(2,1)S(1)}, u32[]{:S(2)}, u32[]{:S(2)}) %collective-permute-start.20) | collective-permute-done | bytes 393248 | tf_op jit(solution)/shard_map/ppermute | solution.py:672
  82.3 3.3 %assemble.1 = (bf16[2,24,64,256]{3,2,1,0:T(8,128)(2,1)S(1)}, bf16[2,6,256,256]{3,2,1,0:T(8,128)(2,1)S(1)}) custom-call(s32[7,27]{1,0:T(8,128)S(1)} %copy-done.1, bf16[12,64,256]{2,1,0:T(8,128)(2,1)S(1)} %copy-done.3, bf16[12,64,256]{2,1,0:T(8,128)(2,1)S(1)} %copy-done.4, bf16[12,64,256]{2,1,0:T(8,128)(2,1)S(1)} %collective-permute-done.15.refs_2_, ...), custom_call_target="tpu_custom_call" | custom-call | tf_op jit(solution)/shard_map/assemble/pallas_call | solution.py:258
  93.9 24.2 %collective-permute-done.25.refs_5_ = bf16[64,6144]{1,0:T(8,128)(2,1)S(1)} collective-permute-done((bf16[64,6144]{1,0:T(8,128)(2,1)S(1)}, bf16[64,6144]{1,0:T(8,128)(2,1)S(1)}, u32[]{:S(2)}, u32[]{:S(2)}) %collective-permute-start.25) | collective-permute-done | bytes 786464 | tf_op jit(solution)/shard_map/ppermute | solution.py:718
  118.1 2.8 %stage.11 = (bf16[64,6144]{1,0:T(8,128)(2,1)S(1)}, bf16[192,3072]{1,0:T(8,128)(2,1)S(1)}, bf16[192,5632]{1,0:T(8,128)(2,1)S(1)}, f32[3,8,1536]{2,1,0:T(8,128)S(1)}, bf16[64,3072]{1,0:T(8,128)(2,1)S(1)}) custom-call(s32[7,27]{1,0:T(8,128)S(1)} %copy-done.1, ...), custom_call_target="tpu_custom_call", output_to_operand_aliasing={{1}: (7, {}), {2}: (8, {}), {3}: (9, {}), {4}: (10, {})} | custom-call | flops 805306368 | bytes 1572864 | tf_op jit(solution)/shard_map/stage/pallas_call | solution.py:448
  122.2 4.5 %collective-permute-done.27.refs_5_ = bf16[64,6144]{1,0:T(8,128)(2,1)S(1)} collective-permute-done((bf16[64,6144]{1,0:T(8,128)(2,1)S(1)}, bf16[64,6144]{1,0:T(8,128)(2,1)S(1)}, u32[]{:S(2)}, u32[]{:S(2)}) %collective-permute-start.27) | collective-permute-done | bytes 786464 | tf_op jit(solution)/shard_map/ppermute | solution.py:718
  126.7 2.6 %stage.12 = (bf16[64,6144]{1,0:T(8,128)(2,1)S(1)}, bf16[192,3072]{1,0:T(8,128)(2,1)S(1)}, bf16[192,5632]{1,0:T(8,128)(2,1)S(1)}, f32[3,8,1536]{2,1,0:T(8,128)S(1)}) custom-call(s32[7,27]{1,0:T(8,128)S(1)} %copy-done.1, bf16[2,1536]{1,0:T(2,128)(2,1)S(1)} %bitcast.13, ...), custom_call_target="tpu_custom_call", output_to_operand_aliasing={{1}: (7, {}), {2}: (8, {}), {3}: (9, {})} | custom-call | flops 805306368 | bytes 1572864 | tf_op jit(solution)/shard_map/stage/pallas_call | solution.py:448
  129.3 1.3 collective-permute-start.29
  130.6 4.8 %collective-permute-done.29.refs_5_ = bf16[64,6144]{1,0:T(8,128)(2,1)S(1)} collective-permute-done((bf16[64,6144]{1,0:T(8,128)(2,1)S(1)}, bf16[64,6144]{1,0:T(8,128)(2,1)S(1)}, u32[]{:S(2)}, u32[]{:S(2)}) %collective-permute-start.29) | collective-permute-done | bytes 786464 | tf_op jit(solution)/shard_map/ppermute | solution.py:718
  135.4 3.5 %stage.13 = (bf16[64,6144]{1,0:T(8,128)(2,1)}, bf16[192,3072]{1,0:T(8,128)(2,1)S(1)}, bf16[192,5632]{1,0:T(8,128)(2,1)S(1)}, f32[3,8,1536]{2,1,0:T(8,128)S(1)}) custom-call(s32[7,27]{1,0:T(8,128)S(1)} %copy-done.1, bf16[2,1536]{1,0:T(2,128)(2,1)S(1)} %bitcast.14, ...), custom_call_target="tpu_custom_call", output_to_operand_aliasing={{1}: (6, {}), {2}: (7, {}), {3}: (8, {})} | custom-call | flops 805306368 | bytes 1572864 | tf_op jit(solution)/shard_map/stage/pallas_call | solution.py:448
  138.9 6.1 %weight.1 = (bf16[25,64,256]{2,1,0:T(8,128)(2,1)S(1)}, bf16[25,64,256]{2,1,0:T(8,128)(2,1)S(1)}, bf16[25,64,256]{2,1,0:T(8,128)(2,1)S(1)}, bf16[25,64,256]{2,1,0:T(8,128)(2,1)S(1)}, bf16[25,64,256]{2,1,0:T(8,128)(2,1)S(1)}) custom-call(s32[7,27]{1,0:T(8,128)S(1)} %copy-done.1, bf16[192,5632]{1,0:T(8,128)(2,1)S(1)} %get-tuple-element.92.saved_ref, ...), custom_call_target="tpu_custom_call" | custom-call | tf_op jit(solution)/shard_map/weight/pallas_call | solution.py:519
  145.0 2.6 %collective-permute-start.35 = (bf16[25,64,256]{2,1,0:T(8,128)(2,1)S(1)}, bf16[25,64,256]{2,1,0:T(8,128)(2,1)S(1)}, u32[]{:S(2)}, u32[]{:S(2)}) collective-permute-start(bf16[25,64,256]{2,1,0:T(8,128)(2,1)S(1)} %get-tuple-element.98), channel_id=1, source_target_pairs={{0,4},{12,8},{1,5},{13,9},{2,6},{14,10},{3,7},{15,11},{16,20},{28,... | collective-permute-start | bytes 2457608 | tf_op jit(solution)/shard_map/ppermute | solution.py:668
  147.6 1.3 collective-permute-start.33
  150.2 15.9 %collective-permute-done.35 = bf16[25,64,256]{2,1,0:T(8,128)(2,1)S(1)} collective-permute-done((bf16[25,64,256]{2,1,0:T(8,128)(2,1)S(1)}, bf16[25,64,256]{2,1,0:T(8,128)(2,1)S(1)}, u32[]{:S(2)}, u32[]{:S(2)}) %collective-permute-start.35) | collective-permute-done | bytes 819232 | tf_op jit(solution)/shard_map/ppermute | solution.py:668
  166.4 3.7 %collective-permute-start.36 = (bf16[25,64,256]{2,1,0:T(8,128)(2,1)S(1)}, bf16[25,64,256]{2,1,0:T(8,128)(2,1)S(1)}, u32[]{:S(2)}, u32[]{:S(2)}) collective-permute-start(bf16[25,64,256]{2,1,0:T(8,128)(2,1)S(1)} %add_convert_fusion), channel_id=1, source_target_pairs={{0,8},{4,12},{8,0},{12,4},{1,9},{5,13},{9,1},{13,5},{2,10},{6,14},... | collective-permute-start | bytes 2457608 | tf_op jit(solution)/shard_map/ppermute | solution.py:668
  171.3 38.4 %collective-permute-done.32.refs_3_ = bf16[64,3072]{1,0:T(8,128)(2,1)S(1)} collective-permute-done((bf16[64,3072]{1,0:T(8,128)(2,1)S(1)}, bf16[64,3072]{1,0:T(8,128)(2,1)S(1)}, u32[]{:S(2)}, u32[]{:S(2)}) %collective-permute-start.32) | collective-permute-done | bytes 393248 | tf_op jit(solution)/shard_map/ppermute | solution.py:723
  209.7 24.9 %collective-permute-start.30 = (bf16[64,3072]{1,0:T(8,128)(2,1)S(1)}, bf16[64,3072]{1,0:T(8,128)(2,1)S(1)}, u32[]{:S(2)}, u32[]{:S(2)}) collective-permute-start(bf16[64,3072]{1,0:T(8,128)(2,1)S(1)} %get-tuple-element.91.refs_0_), channel_id=1, source_target_pairs={{0,4},{4,8},{8,12},{12,0},{1,5},{5,9},{9,13},{13,1},{2,6},{6,10},{... | collective-permute-start | bytes 1179656 | tf_op jit(solution)/shard_map/ppermute | solution.py:723
  234.7 4.8 %collective-permute-done.31.refs_2_ = bf16[64,3072]{1,0:T(8,128)(2,1)S(1)} collective-permute-done((bf16[64,3072]{1,0:T(8,128)(2,1)S(1)}, bf16[64,3072]{1,0:T(8,128)(2,1)S(1)}, u32[]{:S(2)}, u32[]{:S(2)}) %collective-permute-start.31) | collective-permute-done | bytes 393248 | tf_op jit(solution)/shard_map/ppermute | solution.py:723
  239.9 2.0 output.1
  242.0 1.4 total.1
  (112 shorter events, 25.2 us)
Async XLA Ops:
  0.6 9.8 %collective-permute-start.10 = (bf16[768,128]{1,0:T(8,128)(2,1)}, bf16[768,128]{1,0:T(8,128)(2,1)S(1)}, u32[]{:S(2)}, u32[]{:S(2)}) collective-permute-start(bf16[768,128]{1,0:T(8,128)(2,1)} %rest_0_.3), channel_id=1, source_target_pairs={{1,13},{5,1},{9,5},{13,9},{17,29},{21,17},{25,21},{29,25}} | collective-permute-start | bytes 589832 | tf_op jit(solution)/shard_map/ppermute | solution.py:663
  1.3 10.5 %collective-permute-start.8 = (bf16[768,128]{1,0:T(8,128)(2,1)}, bf16[768,128]{1,0:T(8,128)(2,1)S(1)}, u32[]{:S(2)}, u32[]{:S(2)}) collective-permute-start(bf16[768,128]{1,0:T(8,128)(2,1)} %rest_0_.3), channel_id=1, source_target_pairs={{1,9},{5,13},{9,1},{13,5},{17,25},{21,29},{25,17},{29,21}} | collective-permute-start | bytes 589832 | tf_op jit(solution)/shard_map/ppermute | solution.py:663
  2.0 14.6 %collective-permute-start.6 = (bf16[768,128]{1,0:T(8,128)(2,1)}, bf16[768,128]{1,0:T(8,128)(2,1)S(1)}, u32[]{:S(2)}, u32[]{:S(2)}) collective-permute-start(bf16[768,128]{1,0:T(8,128)(2,1)} %rest_0_.3), channel_id=1, source_target_pairs={{1,5},{5,9},{9,13},{13,1},{17,21},{21,25},{25,29},{29,17}} | collective-permute-start | bytes 589832 | tf_op jit(solution)/shard_map/ppermute | solution.py:663
  7.5 13.8 %collective-permute-start = (bf16[64,3072]{1,0:T(8,128)(2,1)}, bf16[64,3072]{1,0:T(8,128)(2,1)}, u32[]{:S(2)}, u32[]{:S(2)}) collective-permute-start(bf16[64,3072]{1,0:T(8,128)(2,1)} %get-tuple-element.53), channel_id=1, source_target_pairs={{1,13},{5,1},{9,5},{13,9},{17,29},{21,17},{25,21},{29,25}} | collective-permute-start | bytes 1179656 | tf_op jit(solution)/shard_map/ppermute | solution.py:658
  9.0 16.8 %collective-permute-start.1 = (bf16[64,3072]{1,0:T(8,128)(2,1)}, bf16[64,3072]{1,0:T(8,128)(2,1)}, u32[]{:S(2)}, u32[]{:S(2)}) collective-permute-start(bf16[64,3072]{1,0:T(8,128)(2,1)} %get-tuple-element.54), channel_id=1, source_target_pairs={{1,9},{5,13},{9,1},{13,5},{17,25},{21,29},{25,17},{29,21}} | collective-permute-start | bytes 1179656 | tf_op jit(solution)/shard_map/ppermute | solution.py:658
  10.4 16.1 %collective-permute-start.2 = (bf16[64,3072]{1,0:T(8,128)(2,1)}, bf16[64,3072]{1,0:T(8,128)(2,1)}, u32[]{:S(2)}, u32[]{:S(2)}) collective-permute-start(bf16[64,3072]{1,0:T(8,128)(2,1)} %get-tuple-element.55), channel_id=1, source_target_pairs={{1,5},{5,9},{9,13},{13,1},{17,21},{21,25},{25,29},{29,17}} | collective-permute-start | bytes 1179656 | tf_op jit(solution)/shard_map/ppermute | solution.py:658
  12.5 16.9 %collective-permute-start.4 = (bf16[12,64,256]{2,1,0:T(8,128)(2,1)}, bf16[12,64,256]{2,1,0:T(8,128)(2,1)S(1)}, u32[]{:S(2)}, u32[]{:S(2)}) collective-permute-start(bf16[12,64,256]{2,1,0:T(8,128)(2,1)} %get-tuple-element.56.refs_0_), channel_id=1, source_target_pairs={{0,8},{4,12},{8,0},{12,4},{1,9},{5,13},{9,1},{13,5},{2,10},{6,14},... | collective-permute-start | bytes 1179656 | tf_op jit(solution)/shard_map/ppermute | solution.py:668
  19.9 39.2 %collective-permute-start.17 = (bf16[12,64,256]{2,1,0:T(8,128)(2,1)}, bf16[12,64,256]{2,1,0:T(8,128)(2,1)S(1)}, u32[]{:S(2)}, u32[]{:S(2)}) collective-permute-start(bf16[12,64,256]{2,1,0:T(8,128)(2,1)} %get-tuple-element.56.refs_0_), channel_id=1, source_target_pairs={{4,0},{8,4},{12,8},{5,1},{9,5},{13,9},{6,2},{10,6},{14,10},{7,3},{... | collective-permute-start | bytes 1179656 | tf_op jit(solution)/shard_map/ppermute | solution.py:668
  21.3 38.5 %collective-permute-start.15 = (bf16[12,64,256]{2,1,0:T(8,128)(2,1)}, bf16[12,64,256]{2,1,0:T(8,128)(2,1)S(1)}, u32[]{:S(2)}, u32[]{:S(2)}) collective-permute-start(bf16[12,64,256]{2,1,0:T(8,128)(2,1)} %get-tuple-element.56.refs_0_), channel_id=1, source_target_pairs={{0,4},{4,8},{8,12},{1,5},{5,9},{9,13},{2,6},{6,10},{10,14},{3,7},{... | collective-permute-start | bytes 1179656 | tf_op jit(solution)/shard_map/ppermute | solution.py:668
  25.8 5.2 %collective-permute-start.9 = (bf16[768,128]{1,0:T(8,128)(2,1)}, bf16[768,128]{1,0:T(8,128)(2,1)S(1)}, u32[]{:S(2)}, u32[]{:S(2)}) collective-permute-start(bf16[768,128]{1,0:T(8,128)(2,1)} %copy-done.10), channel_id=1, source_target_pairs={{1,3},{5,7},{9,11},{13,15},{17,19},{21,23},{25,27},{29,31}} | collective-permute-start | bytes 589832 | tf_op jit(solution)/shard_map/ppermute | solution.py:664
  26.5 5.2 %collective-permute-start.7 = (bf16[768,128]{1,0:T(8,128)(2,1)S(1)}, bf16[768,128]{1,0:T(8,128)(2,1)S(1)}, u32[]{:S(2)}, u32[]{:S(2)}) collective-permute-start(bf16[768,128]{1,0:T(8,128)(2,1)S(1)} %collective-permute-done.6), channel_id=1, source_target_pairs={{1,3},{5,7},{9,11},{13,15},{17,19},{21,23},{25,27},{29,31}} | collective-permute-start | bytes 589832 | tf_op jit(solution)/shard_map/ppermute | solution.py:664
  29.5 28.3 %collective-permute-start.5 = (bf16[12,64,256]{2,1,0:T(8,128)(2,1)S(1)}, bf16[12,64,256]{2,1,0:T(8,128)(2,1)S(1)}, u32[]{:S(2)}, u32[]{:S(2)}) collective-permute-start(bf16[12,64,256]{2,1,0:T(8,128)(2,1)S(1)} %collective-permute-done.4.refs_6_), channel_id=1, source_target_pairs={{4,0},{8,12},{5,1},{9,13},{6,2},{10,14},{7,3},{11,15},{20,16},{24,... | collective-permute-start | bytes 1179656 | tf_op jit(solution)/shard_map/ppermute | solution.py:668
  31.0 37.0 %collective-permute-start.3 = (bf16[64,3072]{1,0:T(8,128)(2,1)S(1)}, bf16[64,3072]{1,0:T(8,128)(2,1)S(1)}, u32[]{:S(2)}, u32[]{:S(2)}) collective-permute-start(bf16[64,3072]{1,0:T(8,128)(2,1)S(1)} %select_select_fusion), channel_id=1, source_target_pairs={{1,3},{5,7},{9,11},{13,15},{17,19},{21,23},{25,27},{29,31}} | collective-permute-start | bytes 1179656 | tf_op jit(solution)/shard_map/ppermute | solution.py:665
  57.8 3.6 %collective-permute-start.14 = (f32[8,128]{1,0:T(8,128)S(1)}, f32[8,128]{1,0:T(8,128)S(1)}, u32[]{:S(2)}, u32[]{:S(2)}) collective-permute-start(f32[8,128]{1,0:T(8,128)S(1)} %score.1.own_ref), channel_id=1, source_target_pairs={{3,7},{7,11},{11,15},{15,3},{19,23},{23,27},{27,31},{31,19}} | collective-permute-start | bytes 12296 | tf_op jit(solution)/shard_map/ppermute | solution.py:697
  58.4 5.4 %collective-permute-start.13 = (f32[8,128]{1,0:T(8,128)S(1)}, f32[8,128]{1,0:T(8,128)S(1)}, u32[]{:S(2)}, u32[]{:S(2)}) collective-permute-start(f32[8,128]{1,0:T(8,128)S(1)} %score.1.own_ref), channel_id=1, source_target_pairs={{3,11},{7,15},{11,3},{15,7},{19,27},{23,31},{27,19},{31,23}} | collective-permute-start | bytes 12296 | tf_op jit(solution)/shard_map/ppermute | solution.py:697
  59.1 5.4 %collective-permute-start.12 = (f32[8,128]{1,0:T(8,128)S(1)}, f32[8,128]{1,0:T(8,128)S(1)}, u32[]{:S(2)}, u32[]{:S(2)}) collective-permute-start(f32[8,128]{1,0:T(8,128)S(1)} %score.1.own_ref), channel_id=1, source_target_pairs={{3,15},{7,3},{11,7},{15,11},{19,31},{23,19},{27,23},{31,27}} | collective-permute-start | bytes 12296 | tf_op jit(solution)/shard_map/ppermute | solution.py:697
  59.8 14.1 %collective-permute-start.19 = (bf16[12,64,256]{2,1,0:T(8,128)(2,1)S(1)}, bf16[12,64,256]{2,1,0:T(8,128)(2,1)S(1)}, u32[]{:S(2)}, u32[]{:S(2)}) collective-permute-start(bf16[12,64,256]{2,1,0:T(8,128)(2,1)S(1)} %collective-permute-done.4.refs_6_), channel_id=1, source_target_pairs={{0,16},{4,20},{8,24},{12,28},{16,0},{20,4},{24,8},{28,12},{1,17},{... | collective-permute-start | bytes 1179656 | tf_op jit(solution)/shard_map/ppermute | solution.py:672
  61.4 12.5 %collective-permute-start.18 = (bf16[12,64,256]{2,1,0:T(8,128)(2,1)S(1)}, bf16[12,64,256]{2,1,0:T(8,128)(2,1)S(1)}, u32[]{:S(2)}, u32[]{:S(2)}) collective-permute-start(bf16[12,64,256]{2,1,0:T(8,128)(2,1)S(1)} %collective-permute-done.17.refs_4_), channel_id=1, source_target_pairs={{0,16},{4,20},{8,24},{16,0},{20,4},{24,8},{1,17},{5,21},{9,25},{17... | collective-permute-start | bytes 1179656 | tf_op jit(solution)/shard_map/ppermute | solution.py:672
  63.8 10.1 %collective-permute-start.16 = (bf16[12,64,256]{2,1,0:T(8,128)(2,1)S(1)}, bf16[12,64,256]{2,1,0:T(8,128)(2,1)S(1)}, u32[]{:S(2)}, u32[]{:S(2)}) collective-permute-start(bf16[12,64,256]{2,1,0:T(8,128)(2,1)S(1)} %collective-permute-done.15.refs_2_), channel_id=1, source_target_pairs={{4,20},{8,24},{12,28},{20,4},{24,8},{28,12},{5,21},{9,25},{13,29},... | collective-permute-start | bytes 1179656 | tf_op jit(solution)/shard_map/ppermute | solution.py:672
  64.5 17.8 %collective-permute-start.20 = (bf16[12,64,256]{2,1,0:T(8,128)(2,1)S(1)}, bf16[12,64,256]{2,1,0:T(8,128)(2,1)S(1)}, u32[]{:S(2)}, u32[]{:S(2)}) collective-permute-start(bf16[12,64,256]{2,1,0:T(8,128)(2,1)S(1)} %collective-permute-done.5.refs_8_), channel_id=1, source_target_pairs={{0,16},{12,28},{16,0},{28,12},{1,17},{13,29},{17,1},{29,13},{2,18}... | collective-permute-start | bytes 1179656 | tf_op jit(solution)/shard_map/ppermute | solution.py:672
  90.5 3.4 %collective-permute-start.26 = (bf16[64,6144]{1,0:T(8,128)(2,1)S(1)}, bf16[64,6144]{1,0:T(8,128)(2,1)S(1)}, u32[]{:S(2)}, u32[]{:S(2)}) collective-permute-start(bf16[64,6144]{1,0:T(8,128)(2,1)S(1)} %get-tuple-element.72), channel_id=1, source_target_pairs={{2,1},{6,5},{10,9},{14,13},{18,17},{22,21},{26,25},{30,29}} | collective-permute-start | bytes 2359304 | tf_op jit(solution)/shard_map/ppermute | solution.py:718
  91.9 26.2 %collective-permute-start.25 = (bf16[64,6144]{1,0:T(8,128)(2,1)S(1)}, bf16[64,6144]{1,0:T(8,128)(2,1)S(1)}, u32[]{:S(2)}, u32[]{:S(2)}) collective-permute-start(bf16[64,6144]{1,0:T(8,128)(2,1)S(1)} %get-tuple-element.77), channel_id=1, source_target_pairs={{1,0},{5,4},{9,8},{13,12},{17,16},{21,20},{25,24},{29,28}} | collective-permute-start | bytes 2359304 | tf_op jit(solution)/shard_map/ppermute | solution.py:718
  93.2 29.0 %collective-permute-start.28 = (bf16[64,6144]{1,0:T(8,128)(2,1)S(1)}, bf16[64,6144]{1,0:T(8,128)(2,1)S(1)}, u32[]{:S(2)}, u32[]{:S(2)}) collective-permute-start(bf16[64,6144]{1,0:T(8,128)(2,1)S(1)} %get-tuple-element.77), channel_id=1, source_target_pairs={{2,1},{6,5},{10,9},{14,13},{18,17},{22,21},{26,25},{30,29}} | collective-permute-start | bytes 2359304 | tf_op jit(solution)/shard_map/ppermute | solution.py:718
  120.9 5.8 %collective-permute-start.27 = (bf16[64,6144]{1,0:T(8,128)(2,1)S(1)}, bf16[64,6144]{1,0:T(8,128)(2,1)S(1)}, u32[]{:S(2)}, u32[]{:S(2)}) collective-permute-start(bf16[64,6144]{1,0:T(8,128)(2,1)S(1)} %get-tuple-element.82), channel_id=1, source_target_pairs={{1,0},{5,4},{9,8},{13,12},{17,16},{21,20},{25,24},{29,28}} | collective-permute-start | bytes 2359304 | tf_op jit(solution)/shard_map/ppermute | solution.py:718
  129.3 6.1 %collective-permute-start.29 = (bf16[64,6144]{1,0:T(8,128)(2,1)S(1)}, bf16[64,6144]{1,0:T(8,128)(2,1)S(1)}, u32[]{:S(2)}, u32[]{:S(2)}) collective-permute-start(bf16[64,6144]{1,0:T(8,128)(2,1)S(1)} %get-tuple-element.86), channel_id=1, source_target_pairs={{1,0},{5,4},{9,8},{13,12},{17,16},{21,20},{25,24},{29,28}} | collective-permute-start | bytes 2359304 | tf_op jit(solution)/shard_map/ppermute | solution.py:718
  145.0 21.1 %collective-permute-start.35 = (bf16[25,64,256]{2,1,0:T(8,128)(2,1)S(1)}, bf16[25,64,256]{2,1,0:T(8,128)(2,1)S(1)}, u32[]{:S(2)}, u32[]{:S(2)}) collective-permute-start(bf16[25,64,256]{2,1,0:T(8,128)(2,1)S(1)} %get-tuple-element.98), channel_id=1, source_target_pairs={{0,4},{12,8},{1,5},{13,9},{2,6},{14,10},{3,7},{15,11},{16,20},{28,... | collective-permute-start | bytes 2457608 | tf_op jit(solution)/shard_map/ppermute | solution.py:668
  147.6 94.4 %collective-permute-start.33 = (bf16[25,64,256]{2,1,0:T(8,128)(2,1)S(1)}, bf16[25,64,256]{2,1,0:T(8,128)(2,1)S(1)}, u32[]{:S(2)}, u32[]{:S(2)}) collective-permute-start(bf16[25,64,256]{2,1,0:T(8,128)(2,1)S(1)} %get-tuple-element.95), channel_id=1, source_target_pairs={{0,4},{4,8},{8,12},{1,5},{5,9},{9,13},{2,6},{6,10},{10,14},{3,7},{... | collective-permute-start | bytes 2457608 | tf_op jit(solution)/shard_map/ppermute | solution.py:668
  148.9 93.1 %collective-permute-start.34 = (bf16[25,64,256]{2,1,0:T(8,128)(2,1)S(1)}, bf16[25,64,256]{2,1,0:T(8,128)(2,1)S(1)}, u32[]{:S(2)}, u32[]{:S(2)}) collective-permute-start(bf16[25,64,256]{2,1,0:T(8,128)(2,1)S(1)} %get-tuple-element.96), channel_id=1, source_target_pairs={{4,0},{8,4},{12,8},{5,1},{9,5},{13,9},{6,2},{10,6},{14,10},{7,3},{... | collective-permute-start | bytes 2457608 | tf_op jit(solution)/shard_map/ppermute | solution.py:668
  166.4 75.6 %collective-permute-start.36 = (bf16[25,64,256]{2,1,0:T(8,128)(2,1)S(1)}, bf16[25,64,256]{2,1,0:T(8,128)(2,1)S(1)}, u32[]{:S(2)}, u32[]{:S(2)}) collective-permute-start(bf16[25,64,256]{2,1,0:T(8,128)(2,1)S(1)} %add_convert_fusion), channel_id=1, source_target_pairs={{0,8},{4,12},{8,0},{12,4},{1,9},{5,13},{9,1},{13,5},{2,10},{6,14},... | collective-permute-start | bytes 2457608 | tf_op jit(solution)/shard_map/ppermute | solution.py:668
  170.1 39.6 %collective-permute-start.32 = (bf16[64,3072]{1,0:T(8,128)(2,1)S(1)}, bf16[64,3072]{1,0:T(8,128)(2,1)S(1)}, u32[]{:S(2)}, u32[]{:S(2)}) collective-permute-start(bf16[64,3072]{1,0:T(8,128)(2,1)S(1)} %get-tuple-element.91.refs_0_), channel_id=1, source_target_pairs={{0,12},{4,0},{8,4},{12,8},{1,13},{5,1},{9,5},{13,9},{2,14},{6,2},{... | collective-permute-start | bytes 1179656 | tf_op jit(solution)/shard_map/ppermute | solution.py:723
  171.3 68.1 %collective-permute-start.31 = (bf16[64,3072]{1,0:T(8,128)(2,1)S(1)}, bf16[64,3072]{1,0:T(8,128)(2,1)S(1)}, u32[]{:S(2)}, u32[]{:S(2)}) collective-permute-start(bf16[64,3072]{1,0:T(8,128)(2,1)S(1)} %get-tuple-element.91.refs_0_), channel_id=1, source_target_pairs={{0,8},{4,12},{8,0},{12,4},{1,9},{5,13},{9,1},{13,5},{2,10},{6,14},... | collective-permute-start | bytes 1179656 | tf_op jit(solution)/shard_map/ppermute | solution.py:723
  209.7 30.2 %collective-permute-start.30 = (bf16[64,3072]{1,0:T(8,128)(2,1)S(1)}, bf16[64,3072]{1,0:T(8,128)(2,1)S(1)}, u32[]{:S(2)}, u32[]{:S(2)}) collective-permute-start(bf16[64,3072]{1,0:T(8,128)(2,1)S(1)} %get-tuple-element.91.refs_0_), channel_id=1, source_target_pairs={{0,4},{4,8},{8,12},{12,0},{1,5},{5,9},{9,13},{13,1},{2,6},{6,10},{... | collective-permute-start | bytes 1179656 | tf_op jit(solution)/shard_map/ppermute | solution.py:723
  (17 other events, 199.2 us)
where the time goes:
time: 244 us; the launch traced here: 243 us
  waiting for transfers between devices  134 us (55%)
  starting transfers between devices  73.6 us (30%)
  Pallas kernels  29.1 us (12%)
  between operations  3.76 us (2%)
    ppermute x3, waiting for transfers between devices, device_program(): lax.ppermute(piece, 'dp', shift_pairs(k))  43.7 us
    ppermute x8, waiting for transfers between devices, along(): return lax.ppermute(array, 'dp', pairs)  43.5 us
    ppermute x9, waiting for transfers between devices, device_program(): table[slot] = lax.ppermute(packet, 'section', hops)  33.4 us
    ppermute x3, starting transfers between devices, device_program(): lax.ppermute(piece, 'dp', shift_pairs(k))  26.1 us
    ppermute x8, starting transfers between devices, along(): return lax.ppermute(array, 'dp', pairs)  20.1 us
    ppermute x4, waiting for transfers between devices, across(): return lax.ppermute(array, ('groups', 'dp'), pairs)  13.6 us
    pallas_call x7, Pallas kernels, stage_call(): pl.pallas_call(functools.partial(stage_kernel, slot, held, len(shapes) -...  11.5 us
    ppermute x9, starting transfers between devices, device_program(): table[slot] = lax.ppermute(packet, 'section', hops)  8.14 us
  transfers between devices with their start and end apart: 37, of which 11 were waited for; matrix products, arithmetic and copies ran while one was open for 1% of the time, Pallas kernels for 5%

commit v1 on v0

--- a/solution.py
+++ b/solution.py
@@ -222,7 +222,7 @@
 
 
 def assemble_kernel(plan, meta_ref, *refs):
-    pieces, (down_ref, up_ref, sem) = refs[: len(plan)], refs[len(plan) :]
+    pieces, (down_ref, up_ref, sem) = refs[: len(plan)], refs[-3:]
     spans = up_ref.shape[1]
 
     def each(action):
@@ -252,7 +252,7 @@
     each(lambda copy: copy.wait())
 
 
-def assemble_call(meta, pieces, plan, half):
+def assemble_call(meta, pieces, plan, half, held=()):
     rank = pieces[0].shape[2]
     part = pieces[0].shape[1]
     return pl.pallas_call(
@@ -260,7 +260,7 @@
         grid_spec=pltpu.PrefetchScalarGridSpec(
             num_scalar_prefetch=1,
             grid=(1,),
-            in_specs=[ANY] * len(pieces),
+            in_specs=[ANY] * len(pieces) + [VMEM] * len(held),
             out_specs=[VMEM] * 2,
             scratch_shapes=[pltpu.SemaphoreType.DMA((2 * len(pieces),))],
         ),
@@ -268,42 +268,53 @@
             jax.ShapeDtypeStruct((2, half // part, part, rank), BF16),
             jax.ShapeDtypeStruct((2, half // rank, rank, rank), BF16),
         ],
+        input_output_aliases={1 + len(pieces) + i: i for i in range(len(held))},
         compiler_params=pltpu.CompilerParams(vmem_limit_bytes=8 << 20),
         name="assemble",
-    )(meta, *pieces)
-
-
-def output_kernel(unit, meta_ref, kept_ref, pairs_ref, *refs):
-    pieces, (out_ref, zero_s, sem) = refs[:QUAD], refs[QUAD:]
+    )(meta, *pieces, *held)
+
+
+def output_kernel(unit, plan, meta_ref, kept_ref, pairs_ref, *refs):
+    pieces, (out_ref, zero_s, sem) = refs[: len(plan)], refs[len(plan) :]
     chunk = pieces[0].shape[0]
     own = pltpu.make_async_copy(
-        pairs_ref.at[pl.ds(chunk, unit)], out_ref.at[pl.ds(0, unit)], sem.at[QUAD]
+        pairs_ref.at[pl.ds(chunk, unit)], out_ref.at[pl.ds(0, unit)], sem.at[len(plan)]
     )
     own.start()
     long = kept_ref[meta_ref[0, 5]] > unit
-    zero_s[...] = jnp.zeros_like(zero_s)
-    for k, piece in enumerate(pieces):
-        start = pl.multiple_of(meta_ref[0, 23 + k], chunk)
-        goal = out_ref.at[pl.ds(start, chunk)]
-
-        @pl.when(long)
-        def _():
-            pltpu.make_async_copy(piece, goal, sem.at[k]).start()
-
-        @pl.when(jnp.logical_not(long))
-        def _():
-            pltpu.make_async_copy(zero_s, goal, sem.at[k]).start()
-
-    for k in range(QUAD):
-        start = pl.multiple_of(meta_ref[0, 23 + k], chunk)
-        pltpu.make_async_copy(zero_s, out_ref.at[pl.ds(start, chunk)], sem.at[k]).wait()
+
+    @pl.when(jnp.logical_not(long))
+    def _():
+        zero_s[...] = jnp.zeros_like(zero_s)
+        copies = [
+            pltpu.make_async_copy(
+                zero_s, out_ref.at[pl.ds(unit + chunk * j, chunk)], sem.at[j]
+            )
+            for j in range(QUAD)
+        ]
+        for copy in copies:
+            copy.start()
+        for copy in copies:
+            copy.wait()
+
+    def each(action):
+        for number, (piece, (place_field, valid_field)) in enumerate(zip(pieces, plan)):
+            start = pl.multiple_of(unit + chunk * meta_ref[0, place_field], chunk)
+            copy = pltpu.make_async_copy(piece, out_ref.at[pl.ds(start, chunk)], sem.at[number])
+
+            @pl.when(jnp.logical_and(long, meta_ref[0, valid_field] == 1))
+            def _():
+                action(copy)
+
+    each(lambda copy: copy.start())
+    each(lambda copy: copy.wait())
     own.wait()
 
 
-def output_call(meta, kept, pairs, pieces, slots):
+def output_call(meta, kept, pairs, pieces, plan, slots):
     chunk, width = pieces[0].shape
     return pl.pallas_call(
-        functools.partial(output_kernel, slots // LONG),
+        functools.partial(output_kernel, slots // LONG, plan),
         grid_spec=pltpu.PrefetchScalarGridSpec(
             num_scalar_prefetch=2,
             grid=(1,),
@@ -311,7 +322,7 @@
             out_specs=ANY,
             scratch_shapes=[
                 pltpu.VMEM((chunk, width), BF16),
-                pltpu.SemaphoreType.DMA((QUAD + 1,)),
+                pltpu.SemaphoreType.DMA((len(plan) + 1,)),
             ],
         ),
         out_shape=jax.ShapeDtypeStruct((slots, width), BF16),
@@ -320,10 +331,12 @@
     )(meta, kept, pairs, *pieces)
 
 
-def stage_kernel(slot, held, firsts, *refs):
+def stage_kernel(slot, held, firsts, kept_state, last, *refs):
     meta_ref, gain_ref, top_ref, down_s, up_s = refs[:5]
     arrived = dict(zip(held, refs[5 : 5 + len(held)]))
-    rest = refs[5 + len(held) + (3 + firsts if slot else 0) :]
+    rest = refs[5 + len(held) + kept_state :]
+    if last:
+        rest = rest[-1:] + rest[:-1]
     packet_ref, pairs_ref, saved_ref, sums_ref = rest[:4]
     first_ref = rest[4] if firsts else None
     packet_s, packet_sem = rest[4 + firsts :]
@@ -438,32 +451,37 @@
                 first_ref[...] = packet_ref[:, width:]
 
 
-def stage_call(slot, meta, gains, top, weights, arrived, state, shapes):
+def stage_call(slot, meta, gains, top, weights, arrived, state, shapes, chunk, last):
     _, wide = top.shape
     half, rank = wide // 4, weights[0].shape[3]
-    rows = shapes[-1].shape[0]
+    rows = chunk
     held = tuple(arrived)
     n_in = 5 + len(held)
-    shapes = shapes[: len(state)] if slot else shapes
-    packet, *state = pl.pallas_call(
-        functools.partial(stage_kernel, slot, held, len(shapes) - 3),
+    packet = jax.ShapeDtypeStruct((rows, wide), BF16)
+    outs = shapes if last else [packet] + shapes
+    scratch = [pltpu.VMEM(packet.shape, BF16), pltpu.SemaphoreType.DMA((4,))]
+    scratch += [pltpu.VMEM(packet.shape, BF16)] if last else []
+    shift = len(outs) - len(shapes)
+    outs = pl.pallas_call(
+        functools.partial(stage_kernel, slot, held, len(shapes) - 3, len(state), last),
         grid_spec=pltpu.PrefetchScalarGridSpec(
             num_scalar_prefetch=1,
             grid=(1,),
             in_specs=[pl.BlockSpec(gains.shape, lambda *_: (0, 0)), ANY]
             + [VMEM] * (2 + len(held) + len(state)),
-            out_specs=[VMEM] * (1 + len(shapes)),
-            scratch_shapes=[pltpu.VMEM((rows, wide), BF16), pltpu.SemaphoreType.DMA((4,))],
-        ),
-        out_shape=[jax.ShapeDtypeStruct((rows, wide), BF16)] + shapes,
-        input_output_aliases={n_in + i: 1 + i for i in range(len(state))},
+            out_specs=[VMEM] * len(outs),
+            scratch_shapes=scratch,
+        ),
+        out_shape=outs,
+        input_output_aliases={n_in + i: shift + i for i in range(len(state))},
         cost_estimate=pl.CostEstimate(
             flops=16 * 2 * rows * half * rank, transcendentals=0, bytes_accessed=4 * rows * wide
         ),
         compiler_params=pltpu.CompilerParams(vmem_limit_bytes=6 << 20),
         name="stage",
     )(meta, gains, top, *weights, *arrived.values(), *state)
-    return packet, state
+    outs = list(outs)
+    return (None, outs) if last else (outs[0], outs[1:])
 
 
 def weight_kernel(fields, meta_ref, saved_ref, first_ref, sums_ref, *refs):
@@ -640,7 +658,7 @@
         1,
     ]
     fields += [unit + chunk * ((place + k) % QUAD) for k in range(1, QUAD)]
-    fields += [unit + chunk * ((place - k) % QUAD) for k in range(QUAD)]
+    fields += [(place - k) % QUAD for k in range(QUAD)]
     meta = jnp.stack(
         [jnp.broadcast_to(jnp.asarray(f).astype(jnp.int32), (count,)) for f in fields], axis=1
     )
@@ -660,8 +678,7 @@
     if direct:
         head_pieces = [head_proj]
         for k in range(1, QUAD):
-            piece = lax.ppermute(head_proj, ("dp", "section"), shift_pairs(k, via))
-            head_pieces.append(lax.ppermute(piece, "section", [(via, top)]))
+            head_pieces.append(lax.ppermute(head_proj, ("dp", "section"), shift_pairs(k, top)))
         dealt = lax.ppermute(dealt, "section", [(via, top)])
 
         def along(array, pairs):
@@ -675,9 +692,6 @@
         left = along(mine_msg, [(1, 0), (2, 1), (3, 2)])
         far = along(mine_msg, [(0, 2), (1, 3), (2, 0), (3, 1)])
         relay = along(far, [(1, 0), (2, 3)])
-        gain_row, out_row = head_gain[None], head_out[None]
-        coef = score_call(meta, kept, teacher, top_pair, gain_row, out_row, head_pieces, unit)
-        relay, coef = lax.optimization_barrier((relay, coef))
         for piece, place_field, valid_field, valid in (
             (right, 12, 16, (1, 2, 3)),
             (left, 13, 17, (0, 1, 2)),
@@ -689,9 +703,8 @@
     else:
         head_pieces = [lax.all_gather(head_proj, "dp", axis=0, tiled=True)]
 
-    if not direct:
-        gain_row, out_row = head_gain[None], head_out[None]
-        coef = score_call(meta, kept, teacher, top_pair, gain_row, out_row, head_pieces, unit)
+    gain_row, out_row = head_gain[None], head_out[None]
+    coef = score_call(meta, kept, teacher, top_pair, gain_row, out_row, head_pieces, unit)
     far_coef = coef
     for k in range(1, QUAD):
         other = lax.ppermute(coef, ("dp", "section"), shift_pairs(k, top))
@@ -705,14 +718,20 @@
         jax.ShapeDtypeStruct((chunk, width), BF16),
     ]
     state = []
-    weights = assemble_call(meta, pieces, plan, half)
+    weights = assemble_call(meta, pieces[:8], plan[:8], half)
+    if direct:
+        weights = assemble_call(meta, pieces[8:], plan[8:], half, weights)
     near, far_in = {}, {}
     for slot in range(count):
         arrived = {1: near.get(slot - 1), 2: far_in.get(slot - 2)}
         arrived = {kind: array for kind, array in arrived.items() if array is not None}
-        packet, state = stage_call(slot, meta, gains[0], packets, weights, arrived, state, shapes)
+        if slot > offsets[0]:
+            shapes = shapes[:3]
+        packet, state = stage_call(
+            slot, meta, gains[0], packets, weights, arrived, state, shapes, chunk, slot == count - 1
+        )
         live = [s for s in range(1, sections) if 0 <= slot - offsets[s] < micros]
-        for table, odd in ((near, 1), (far_in, 0)):
+        for table, odd in ((far_in, 0), (near, 1)):
             hops = [(s, s - 1) for s in live if s % 2 == odd]
             if hops:
                 table[slot] = lax.ppermute(packet, "section", hops)
@@ -720,19 +739,28 @@
             piece = state.pop()
     pairs, saved, sums = state
 
-    returned = [piece] + [lax.ppermute(piece, "dp", shift_pairs(k)) for k in range(1, QUAD)]
-    grads_out = output_call(meta, kept, pairs, returned, slots)
+    returned, home_plan = [piece], [(23, 19)]
+    if direct:
+        far_home = along(piece, [(0, 2), (1, 3), (2, 0), (3, 1)])
+        returned += [along(piece, [(0, 1), (1, 2), (2, 3)]), along(piece, [(1, 0), (2, 1), (3, 2)])]
+        returned += [far_home, along(far_home, [(1, 0), (2, 3)])]
+        home_plan += [(12, 16), (13, 17), (14, 19), (15, 18)]
+    else:
+        for k in range(1, QUAD):
+            returned.append(lax.ppermute(piece, "dp", shift_pairs(k)))
+            home_plan.append((23 + k, 19))
+    grads_out = output_call(meta, kept, pairs, returned, home_plan, slots)
 
     if direct:
         own_w, right_w, left_w, far_w, relay_w = weight_call(
             meta, saved, pairs, sums, (7, 13, 12, 14, 15), parts, half, rank
         )
         handed = along(relay_w, [(0, 1), (3, 2)])
+        outer = along(far_w, [(0, 2), (3, 1)])
         from_left = along(right_w, [(0, 1), (1, 2), (2, 3)])
         from_right = along(left_w, [(1, 0), (2, 1), (3, 2)])
-        far_w = (far_w.astype(F32) + handed.astype(F32)).astype(BF16)
-        from_far = along(far_w, [(0, 2), (1, 3), (2, 0), (3, 1)])
-        messages = [own_w, from_left, from_right, from_far]
+        inner = along((far_w.astype(F32) + handed.astype(F32)).astype(BF16), [(1, 3), (2, 0)])
+        messages = [own_w, from_left, from_right, outer, inner]
         down_sum, up_sum, gain_sum = total_call(messages, 1.0 / devices, half)
     else:
         (whole,) = weight_call(meta, saved, pairs, sums, (7,), parts, half, rank)

time: 244 us -> 235 us (0.963)
  starting transfers between devices: 73.6 us -> 59.5 us
  waiting for transfers between devices: 134 us -> 138 us
    ppermute x8 -> x13, waiting for transfers between devices: 43.5 us -> 107 us  [along(): return lax.ppermute(array, 'dp', pairs)]
    ppermute x9 -> x3, waiting for transfers between devices: 43.7 us -> 0.01 us  [device_program(): lax.ppermute(head_proj, ('dp', 'section'), shift_pairs(k, top))]
    ppermute x9 -> x3, starting transfers between devices: 30.2 us -> 2.01 us  [device_program(): lax.ppermute(head_proj, ('dp', 'section'), shift_pairs(k, top))]
    ppermute x8 -> x13, starting transfers between devices: 20.1 us -> 34.4 us  [along(): return lax.ppermute(array, 'dp', pairs)]
    ppermute x9, waiting for transfers between devices: 33.4 us -> 24.9 us  [device_program(): table[slot] = lax.ppermute(packet, 'section', hops)]
    ppermute x4, waiting for transfers between devices: 13.6 us -> 6.13 us  [across(): return lax.ppermute(array, ('groups', 'dp'), pairs)]
  transfers between devices with their start and end apart: 37 -> 36, of which waited for: 11 -> 12; matrix products, arithmetic and copies ran while one was open for 1% -> 1% of each run, Pallas kernels for 5% -> 4%
where the time goes in v1:
time: 235 us; the launch traced here: 234 us
  waiting for transfers between devices  138 us (59%)
  starting transfers between devices  59.5 us (25%)
  Pallas kernels  28.7 us (12%)
  between operations  3.85 us (2%)
    ppermute x13, waiting for transfers between devices, along(): return lax.ppermute(array, 'dp', pairs)  107 us
    ppermute x13, starting transfers between devices, along(): return lax.ppermute(array, 'dp', pairs)  34.4 us
    ppermute x9, waiting for transfers between devices, device_program(): table[slot] = lax.ppermute(packet, 'section', hops)  24.9 us
    pallas_call x7, Pallas kernels, stage_call(): pl.pallas_call(functools.partial(stage_kernel, slot, held, len(shapes) -...  10.3 us
    ppermute x9, starting transfers between devices, device_program(): table[slot] = lax.ppermute(packet, 'section', hops)  8.14 us
    ppermute x4, starting transfers between devices, across(): return lax.ppermute(array, ('groups', 'dp'), pairs)  8.04 us
    ppermute x4, waiting for transfers between devices, across(): return lax.ppermute(array, ('groups', 'dp'), pairs)  6.13 us
    pallas_call x1, Pallas kernels, weight_call(): pl.pallas_call(functools.partial(weight_kernel, fields), grid_spec=pltpu....  6.1 us
  transfers between devices with their start and end apart: 36, of which 12 were waited for; matrix products, arithmetic and copies ran while one was open for 1% of the time, Pallas kernels for 4%

profile of v1, /device:TPU:0, one launch (start us, length us, event | category | flops | bytes accessed | tf_op | source)
XLA Modules:
  0.0 234.4 jit_solution(10989748491211415136)
XLA Ops:
  2.0 3.4 %pack.1 = (bf16[12,64,256]{2,1,0:T(8,128)(2,1)}, bf16[12,64,256]{2,1,0:T(8,128)(2,1)}, bf16[64,3072]{1,0:T(8,128)(2,1)}, bf16[64,3072]{1,0:T(8,128)(2,1)}, bf16[64,3072]{1,0:T(8,128)(2,1)}) custom-call(s32[7,27]{1,0:T(8,128)} %stack.2.meta_ref.refs_0_, bf16[2,6,64,256]{3,2,1,0:T(8,128)(2,1)} %bitcast.18, bf16[2,64,1536]{2,1,0:T(8,128)(2,1)} %bitcast.19, ...), custom_call_target="tpu_custom_call" | custom-call | tf_op jit(solution)/shard_map/pack/pallas_call | solution.py:205
  5.4 5.8 %collective-permute-start.13 = (bf16[12,64,256]{2,1,0:T(8,128)(2,1)}, bf16[12,64,256]{2,1,0:T(8,128)(2,1)}, u32[]{:S(2)}, u32[]{:S(2)}) collective-permute-start(bf16[12,64,256]{2,1,0:T(8,128)(2,1)} %get-tuple-element.56.refs_0_), channel_id=1, source_target_pairs={{0,4},{4,8},{8,12},{1,5},{5,9},{9,13},{2,6},{6,10},{10,14},{3,7},{... | collective-permute-start | bytes 1179656 | tf_op jit(solution)/shard_map/ppermute | solution.py:685
  17.5 3.0 %collective-permute-start.10 = (bf16[12,64,256]{2,1,0:T(8,128)(2,1)S(1)}, bf16[12,64,256]{2,1,0:T(8,128)(2,1)}, u32[]{:S(2)}, u32[]{:S(2)}) collective-permute-start(bf16[12,64,256]{2,1,0:T(8,128)(2,1)S(1)} %copy-done.3), channel_id=1, source_target_pairs={{0,8},{4,12},{8,0},{12,4},{1,9},{5,13},{9,1},{13,5},{2,10},{6,14},... | collective-permute-start | bytes 1179656 | tf_op jit(solution)/shard_map/ppermute | solution.py:685
  20.5 1.4 collective-permute-start
  22.5 1.4 collective-permute-start.1
  23.9 1.4 collective-permute-start.2
  28.7 2.7 %collective-permute-done.15.refs_4_ = bf16[12,64,256]{2,1,0:T(8,128)(2,1)} collective-permute-done((bf16[12,64,256]{2,1,0:T(8,128)(2,1)S(1)}, bf16[12,64,256]{2,1,0:T(8,128)(2,1)}, u32[]{:S(2)}, u32[]{:S(2)}) %collective-permute-start.15) | collective-permute-done | bytes 393248 | tf_op jit(solution)/shard_map/ppermute | solution.py:685
  32.0 23.7 %collective-permute-done.10.refs_6_ = bf16[12,64,256]{2,1,0:T(8,128)(2,1)} collective-permute-done((bf16[12,64,256]{2,1,0:T(8,128)(2,1)S(1)}, bf16[12,64,256]{2,1,0:T(8,128)(2,1)}, u32[]{:S(2)}, u32[]{:S(2)}) %collective-permute-start.10) | collective-permute-done | bytes 393248 | tf_op jit(solution)/shard_map/ppermute | solution.py:685
  55.8 1.5 collective-permute-start.17
  59.3 2.4 %collective-permute-start.16 = (bf16[12,64,256]{2,1,0:T(8,128)(2,1)}, bf16[12,64,256]{2,1,0:T(8,128)(2,1)S(1)}, u32[]{:S(2)}, u32[]{:S(2)}) collective-permute-start(bf16[12,64,256]{2,1,0:T(8,128)(2,1)} %collective-permute-done.15.refs_4_), channel_id=1, source_target_pairs={{0,16},{4,20},{8,24},{16,0},{20,4},{24,8},{1,17},{5,21},{9,25},{17... | collective-permute-start | bytes 1179656 | tf_op jit(solution)/shard_map/ppermute | solution.py:689
  62.6 8.4 %collective-permute-done.11.refs_0_ = bf16[12,64,256]{2,1,0:T(8,128)(2,1)S(1)} collective-permute-done((bf16[12,64,256]{2,1,0:T(8,128)(2,1)}, bf16[12,64,256]{2,1,0:T(8,128)(2,1)S(1)}, u32[]{:S(2)}, u32[]{:S(2)}) %collective-permute-start.11) | collective-permute-done | bytes 393248 | tf_op jit(solution)/shard_map/ppermute | solution.py:685
  71.1 3.4 %collective-permute-start.12 = (bf16[12,64,256]{2,1,0:T(8,128)(2,1)S(1)}, bf16[12,64,256]{2,1,0:T(8,128)(2,1)S(1)}, u32[]{:S(2)}, u32[]{:S(2)}) collective-permute-start(bf16[12,64,256]{2,1,0:T(8,128)(2,1)S(1)} %collective-permute-done.11.refs_0_), channel_id=1, source_target_pairs={{0,16},{12,28},{16,0},{28,12},{1,17},{13,29},{17,1},{29,13},{2,18}... | collective-permute-start | bytes 1179656 | tf_op jit(solution)/shard_map/ppermute | solution.py:689
  74.6 2.8 %assemble.2 = (bf16[2,24,64,256]{3,2,1,0:T(8,128)(2,1)S(1)}, bf16[2,6,256,256]{3,2,1,0:T(8,128)(2,1)S(1)}) custom-call(s32[7,27]{1,0:T(8,128)S(1)} %copy-done.1, bf16[12,64,256]{2,1,0:T(8,128)(2,1)S(1)} %copy-done.3, bf16[12,64,256]{2,1,0:T(8,128)(2,1)S(1)} %copy-done.4, bf16[12,64,256]{2,1,0:T(8,128)(2,1)} %collective-permute-done.13.refs_2_, ...), custom_call_target="tpu_custom_call" | custom-call | tf_op jit(solution)/shard_map/assemble/pallas_call | solution.py:258
  78.1 6.1 %collective-permute-done.12.refs_1_ = bf16[12,64,256]{2,1,0:T(8,128)(2,1)S(1)} collective-permute-done((bf16[12,64,256]{2,1,0:T(8,128)(2,1)S(1)}, bf16[12,64,256]{2,1,0:T(8,128)(2,1)S(1)}, u32[]{:S(2)}, u32[]{:S(2)}) %collective-permute-start.12) | collective-permute-done | bytes 393248 | tf_op jit(solution)/shard_map/ppermute | solution.py:689
  93.7 15.6 %collective-permute-done.22.refs_5_ = bf16[64,6144]{1,0:T(8,128)(2,1)S(1)} collective-permute-done((bf16[64,6144]{1,0:T(8,128)(2,1)S(1)}, bf16[64,6144]{1,0:T(8,128)(2,1)S(1)}, u32[]{:S(2)}, u32[]{:S(2)}) %collective-permute-start.22) | collective-permute-done | bytes 786464 | tf_op jit(solution)/shard_map/ppermute | solution.py:737
  109.3 2.7 %stage.11 = (bf16[64,6144]{1,0:T(8,128)(2,1)S(1)}, bf16[192,3072]{1,0:T(8,128)(2,1)S(1)}, bf16[192,5632]{1,0:T(8,128)(2,1)S(1)}, f32[3,8,1536]{2,1,0:T(8,128)S(1)}, bf16[64,3072]{1,0:T(8,128)(2,1)S(1)}) custom-call(s32[7,27]{1,0:T(8,128)S(1)} %copy-done.1, ...), custom_call_target="tpu_custom_call", output_to_operand_aliasing={{1}: (7, {}), {2}: (8, {}), {3}: (9, {}), {4}: (10, {})} | custom-call | flops 805306368 | bytes 1572864 | tf_op jit(solution)/shard_map/stage/pallas_call | solution.py:465
  113.4 4.6 %collective-permute-done.24.refs_5_ = bf16[64,6144]{1,0:T(8,128)(2,1)S(1)} collective-permute-done((bf16[64,6144]{1,0:T(8,128)(2,1)S(1)}, bf16[64,6144]{1,0:T(8,128)(2,1)S(1)}, u32[]{:S(2)}, u32[]{:S(2)}) %collective-permute-start.24) | collective-permute-done | bytes 786464 | tf_op jit(solution)/shard_map/ppermute | solution.py:737
  117.9 2.5 %stage.12 = (bf16[64,6144]{1,0:T(8,128)(2,1)S(1)}, bf16[192,3072]{1,0:T(8,128)(2,1)S(1)}, bf16[192,5632]{1,0:T(8,128)(2,1)S(1)}, f32[3,8,1536]{2,1,0:T(8,128)S(1)}) custom-call(s32[7,27]{1,0:T(8,128)S(1)} %copy-done.1, bf16[2,1536]{1,0:T(2,128)(2,1)S(1)} %bitcast.13, ...), custom_call_target="tpu_custom_call", output_to_operand_aliasing={{1}: (7, {}), {2}: (8, {}), {3}: (9, {})} | custom-call | flops 805306368 | bytes 1572864 | tf_op jit(solution)/shard_map/stage/pallas_call | solution.py:465
  121.8 4.8 %collective-permute-done.26.refs_5_ = bf16[64,6144]{1,0:T(8,128)(2,1)S(1)} collective-permute-done((bf16[64,6144]{1,0:T(8,128)(2,1)S(1)}, bf16[64,6144]{1,0:T(8,128)(2,1)S(1)}, u32[]{:S(2)}, u32[]{:S(2)}) %collective-permute-start.26) | collective-permute-done | bytes 786464 | tf_op jit(solution)/shard_map/ppermute | solution.py:737
  126.5 2.5 %stage.13 = (bf16[192,3072]{1,0:T(8,128)(2,1)S(1)}, bf16[192,5632]{1,0:T(8,128)(2,1)S(1)}, f32[3,8,1536]{2,1,0:T(8,128)S(1)}) custom-call(s32[7,27]{1,0:T(8,128)S(1)} %copy-done.1, bf16[2,1536]{1,0:T(2,128)(2,1)S(1)} %bitcast.14, bf16[192,6144]{1,0:T(8,128)(2,1)S(1)} %head.1.refs_2_, ...), custom_call_target="tpu_custom_call", output_to_operand_aliasing={{0}: (6, {}), {1}: (7, {}), {2}: (8, {})} | custom-call | flops 805306368 | bytes 1572864 | tf_op jit(solution)/shard_map/stage/pallas_call | solution.py:465
  129.0 6.1 %weight.1 = (bf16[25,64,256]{2,1,0:T(8,128)(2,1)S(1)}, bf16[25,64,256]{2,1,0:T(8,128)(2,1)S(1)}, bf16[25,64,256]{2,1,0:T(8,128)(2,1)S(1)}, bf16[25,64,256]{2,1,0:T(8,128)(2,1)S(1)}, bf16[25,64,256]{2,1,0:T(8,128)(2,1)S(1)}) custom-call(s32[7,27]{1,0:T(8,128)S(1)} %copy-done.1, bf16[192,5632]{1,0:T(8,128)(2,1)S(1)} %get-tuple-element.92.saved_ref, ...), custom_call_target="tpu_custom_call" | custom-call | tf_op jit(solution)/shard_map/weight/pallas_call | solution.py:537
  135.1 7.3 %collective-permute-start.34 = (bf16[25,64,256]{2,1,0:T(8,128)(2,1)S(1)}, bf16[25,64,256]{2,1,0:T(8,128)(2,1)S(1)}, u32[]{:S(2)}, u32[]{:S(2)}) collective-permute-start(bf16[25,64,256]{2,1,0:T(8,128)(2,1)S(1)} %get-tuple-element.98), channel_id=1, source_target_pairs={{0,4},{12,8},{1,5},{13,9},{2,6},{14,10},{3,7},{15,11},{16,20},{28,... | collective-permute-start | bytes 2457608 | tf_op jit(solution)/shard_map/ppermute | solution.py:685
  142.5 2.7 %collective-permute-start.27 = (bf16[64,3072]{1,0:T(8,128)(2,1)S(1)}, bf16[64,3072]{1,0:T(8,128)(2,1)S(1)}, u32[]{:S(2)}, u32[]{:S(2)}) collective-permute-start(bf16[64,3072]{1,0:T(8,128)(2,1)S(1)} %get-tuple-element.91.refs_0_), channel_id=1, source_target_pairs={{0,4},{4,8},{8,12},{1,5},{5,9},{9,13},{2,6},{6,10},{10,14},{3,7},{... | collective-permute-start | bytes 1179656 | tf_op jit(solution)/shard_map/ppermute | solution.py:685
  145.2 4.6 %collective-permute-start.31 = (bf16[25,64,256]{2,1,0:T(8,128)(2,1)S(1)}, bf16[25,64,256]{2,1,0:T(8,128)(2,1)S(1)}, u32[]{:S(2)}, u32[]{:S(2)}) collective-permute-start(bf16[25,64,256]{2,1,0:T(8,128)(2,1)S(1)} %get-tuple-element.95), channel_id=1, source_target_pairs={{0,4},{4,8},{8,12},{1,5},{5,9},{9,13},{2,6},{6,10},{10,14},{3,7},{... | collective-permute-start | bytes 2457608 | tf_op jit(solution)/shard_map/ppermute | solution.py:685
  151.2 9.8 %collective-permute-done.34 = bf16[25,64,256]{2,1,0:T(8,128)(2,1)S(1)} collective-permute-done((bf16[25,64,256]{2,1,0:T(8,128)(2,1)S(1)}, bf16[25,64,256]{2,1,0:T(8,128)(2,1)S(1)}, u32[]{:S(2)}, u32[]{:S(2)}) %collective-permute-start.34) | collective-permute-done | bytes 819232 | tf_op jit(solution)/shard_map/ppermute | solution.py:685
  161.0 3.2 %collective-permute-start.33 = (bf16[25,64,256]{2,1,0:T(8,128)(2,1)S(1)}, bf16[25,64,256]{2,1,0:T(8,128)(2,1)S(1)}, u32[]{:S(2)}, u32[]{:S(2)}) collective-permute-start(bf16[25,64,256]{2,1,0:T(8,128)(2,1)S(1)} %get-tuple-element.97), channel_id=1, source_target_pairs={{0,8},{12,4},{1,9},{13,5},{2,10},{14,6},{3,11},{15,7},{16,24},{28,... | collective-permute-start | bytes 2457608 | tf_op jit(solution)/shard_map/ppermute | solution.py:685
  164.5 5.0 %collective-permute-done.29.refs_3_ = bf16[64,3072]{1,0:T(8,128)(2,1)S(1)} collective-permute-done((bf16[64,3072]{1,0:T(8,128)(2,1)S(1)}, bf16[64,3072]{1,0:T(8,128)(2,1)S(1)}, u32[]{:S(2)}, u32[]{:S(2)}) %collective-permute-start.29) | collective-permute-done | bytes 393248 | tf_op jit(solution)/shard_map/ppermute | solution.py:685
  170.8 7.1 %collective-permute-done.27.refs_1_ = bf16[64,3072]{1,0:T(8,128)(2,1)S(1)} collective-permute-done((bf16[64,3072]{1,0:T(8,128)(2,1)S(1)}, bf16[64,3072]{1,0:T(8,128)(2,1)S(1)}, u32[]{:S(2)}, u32[]{:S(2)}) %collective-permute-start.27) | collective-permute-done | bytes 393248 | tf_op jit(solution)/shard_map/ppermute | solution.py:685
  179.2 12.9 %collective-permute-done.28.refs_2_ = bf16[64,3072]{1,0:T(8,128)(2,1)S(1)} collective-permute-done((bf16[64,3072]{1,0:T(8,128)(2,1)S(1)}, bf16[64,3072]{1,0:T(8,128)(2,1)S(1)}, u32[]{:S(2)}, u32[]{:S(2)}) %collective-permute-start.28) | collective-permute-done | bytes 393248 | tf_op jit(solution)/shard_map/ppermute | solution.py:685
  193.4 37.5 %collective-permute-done.30.refs_4_ = bf16[64,3072]{1,0:T(8,128)(2,1)S(1)} collective-permute-done((bf16[64,3072]{1,0:T(8,128)(2,1)S(1)}, bf16[64,3072]{1,0:T(8,128)(2,1)S(1)}, u32[]{:S(2)}, u32[]{:S(2)}) %collective-permute-start.30) | collective-permute-done | bytes 393248 | tf_op jit(solution)/shard_map/ppermute | solution.py:685
  231.0 2.0 output.1
  233.0 1.4 total.1
  (121 shorter events, 30.5 us)
Async XLA Ops:
  5.4 18.5 %collective-permute-start.13 = (bf16[12,64,256]{2,1,0:T(8,128)(2,1)}, bf16[12,64,256]{2,1,0:T(8,128)(2,1)}, u32[]{:S(2)}, u32[]{:S(2)}) collective-permute-start(bf16[12,64,256]{2,1,0:T(8,128)(2,1)} %get-tuple-element.56.refs_0_), channel_id=1, source_target_pairs={{0,4},{4,8},{8,12},{1,5},{5,9},{9,13},{2,6},{6,10},{10,14},{3,7},{... | collective-permute-start | bytes 1179656 | tf_op jit(solution)/shard_map/ppermute | solution.py:685
  11.3 2.7 %collective-permute-start.4 = (bf16[768,128]{1,0:T(8,128)(2,1)S(1)}, bf16[768,128]{1,0:T(8,128)(2,1)S(1)}, u32[]{:S(2)}, u32[]{:S(2)}) collective-permute-start(bf16[768,128]{1,0:T(8,128)(2,1)S(1)} %copy-done.2), channel_id=1, source_target_pairs={{3,7},{7,11},{11,15},{15,3},{19,23},{23,27},{27,31},{31,19}} | collective-permute-start | bytes 589832 | tf_op jit(solution)/shard_map/ppermute | solution.py:681
  12.0 2.1 collective-permute-start.5
  14.8 5.7 %collective-permute-start.7 = (f32[8,128]{1,0:T(8,128)S(1)}, f32[8,128]{1,0:T(8,128)S(1)}, u32[]{:S(2)}, u32[]{:S(2)}) collective-permute-start(f32[8,128]{1,0:T(8,128)S(1)} %score.1.own_ref), channel_id=1, source_target_pairs={{3,15},{7,3},{11,7},{15,11},{19,31},{23,19},{27,23},{31,27}} | collective-permute-start | bytes 12296 | tf_op jit(solution)/shard_map/ppermute | solution.py:710
  15.5 6.4 %collective-permute-start.8 = (f32[8,128]{1,0:T(8,128)S(1)}, f32[8,128]{1,0:T(8,128)S(1)}, u32[]{:S(2)}, u32[]{:S(2)}) collective-permute-start(f32[8,128]{1,0:T(8,128)S(1)} %score.1.own_ref), channel_id=1, source_target_pairs={{3,11},{7,15},{11,3},{15,7},{19,27},{23,31},{27,19},{31,23}} | collective-permute-start | bytes 12296 | tf_op jit(solution)/shard_map/ppermute | solution.py:710
  16.2 15.2 %collective-permute-start.15 = (bf16[12,64,256]{2,1,0:T(8,128)(2,1)S(1)}, bf16[12,64,256]{2,1,0:T(8,128)(2,1)}, u32[]{:S(2)}, u32[]{:S(2)}) collective-permute-start(bf16[12,64,256]{2,1,0:T(8,128)(2,1)S(1)} %copy-done.3), channel_id=1, source_target_pairs={{4,0},{8,4},{12,8},{5,1},{9,5},{13,9},{6,2},{10,6},{14,10},{7,3},{... | collective-permute-start | bytes 1179656 | tf_op jit(solution)/shard_map/ppermute | solution.py:685
  17.5 38.2 %collective-permute-start.10 = (bf16[12,64,256]{2,1,0:T(8,128)(2,1)S(1)}, bf16[12,64,256]{2,1,0:T(8,128)(2,1)}, u32[]{:S(2)}, u32[]{:S(2)}) collective-permute-start(bf16[12,64,256]{2,1,0:T(8,128)(2,1)S(1)} %copy-done.3), channel_id=1, source_target_pairs={{0,8},{4,12},{8,0},{12,4},{1,9},{5,13},{9,1},{13,5},{2,10},{6,14},... | collective-permute-start | bytes 1179656 | tf_op jit(solution)/shard_map/ppermute | solution.py:685
  20.5 36.8 %collective-permute-start = (bf16[64,3072]{1,0:T(8,128)(2,1)}, bf16[64,3072]{1,0:T(8,128)(2,1)}, u32[]{:S(2)}, u32[]{:S(2)}) collective-permute-start(bf16[64,3072]{1,0:T(8,128)(2,1)} %get-tuple-element.53), channel_id=1, source_target_pairs={{1,13},{5,1},{9,5},{13,9},{17,29},{21,17},{25,21},{29,25}} | collective-permute-start | bytes 1179656 | tf_op jit(solution)/shard_map/ppermute | solution.py:676
  22.5 36.0 %collective-permute-start.1 = (bf16[64,3072]{1,0:T(8,128)(2,1)}, bf16[64,3072]{1,0:T(8,128)(2,1)}, u32[]{:S(2)}, u32[]{:S(2)}) collective-permute-start(bf16[64,3072]{1,0:T(8,128)(2,1)} %get-tuple-element.54), channel_id=1, source_target_pairs={{1,9},{5,13},{9,1},{13,5},{17,25},{21,29},{25,17},{29,21}} | collective-permute-start | bytes 1179656 | tf_op jit(solution)/shard_map/ppermute | solution.py:676
  23.9 35.3 %collective-permute-start.2 = (bf16[64,3072]{1,0:T(8,128)(2,1)}, bf16[64,3072]{1,0:T(8,128)(2,1)}, u32[]{:S(2)}, u32[]{:S(2)}) collective-permute-start(bf16[64,3072]{1,0:T(8,128)(2,1)} %get-tuple-element.55), channel_id=1, source_target_pairs={{1,5},{5,9},{9,13},{13,1},{17,21},{21,25},{25,29},{29,17}} | collective-permute-start | bytes 1179656 | tf_op jit(solution)/shard_map/ppermute | solution.py:676
  31.4 30.6 %collective-permute-start.9 = (f32[8,128]{1,0:T(8,128)}, f32[8,128]{1,0:T(8,128)S(1)}, u32[]{:S(2)}, u32[]{:S(2)}) collective-permute-start(f32[8,128]{1,0:T(8,128)} %copy-done.6), channel_id=1, source_target_pairs={{3,7},{7,11},{11,15},{15,3},{19,23},{23,27},{27,31},{31,19}} | collective-permute-start | bytes 12296 | tf_op jit(solution)/shard_map/ppermute | solution.py:710
  55.8 18.8 %collective-permute-start.17 = (bf16[12,64,256]{2,1,0:T(8,128)(2,1)}, bf16[12,64,256]{2,1,0:T(8,128)(2,1)S(1)}, u32[]{:S(2)}, u32[]{:S(2)}) collective-permute-start(bf16[12,64,256]{2,1,0:T(8,128)(2,1)} %collective-permute-done.10.refs_6_), channel_id=1, source_target_pairs={{0,16},{4,20},{8,24},{12,28},{16,0},{20,4},{24,8},{28,12},{1,17},{... | collective-permute-start | bytes 1179656 | tf_op jit(solution)/shard_map/ppermute | solution.py:689
  57.3 13.8 %collective-permute-start.11 = (bf16[12,64,256]{2,1,0:T(8,128)(2,1)}, bf16[12,64,256]{2,1,0:T(8,128)(2,1)S(1)}, u32[]{:S(2)}, u32[]{:S(2)}) collective-permute-start(bf16[12,64,256]{2,1,0:T(8,128)(2,1)} %collective-permute-done.10.refs_6_), channel_id=1, source_target_pairs={{4,0},{8,12},{5,1},{9,13},{6,2},{10,14},{7,3},{11,15},{20,16},{24,... | collective-permute-start | bytes 1179656 | tf_op jit(solution)/shard_map/ppermute | solution.py:685
  58.6 16.0 %collective-permute-start.14 = (bf16[12,64,256]{2,1,0:T(8,128)(2,1)}, bf16[12,64,256]{2,1,0:T(8,128)(2,1)S(1)}, u32[]{:S(2)}, u32[]{:S(2)}) collective-permute-start(bf16[12,64,256]{2,1,0:T(8,128)(2,1)} %collective-permute-done.13.refs_2_), channel_id=1, source_target_pairs={{4,20},{8,24},{12,28},{20,4},{24,8},{28,12},{5,21},{9,25},{13,29},... | collective-permute-start | bytes 1179656 | tf_op jit(solution)/shard_map/ppermute | solution.py:689
  59.3 15.3 %collective-permute-start.16 = (bf16[12,64,256]{2,1,0:T(8,128)(2,1)}, bf16[12,64,256]{2,1,0:T(8,128)(2,1)S(1)}, u32[]{:S(2)}, u32[]{:S(2)}) collective-permute-start(bf16[12,64,256]{2,1,0:T(8,128)(2,1)} %collective-permute-done.15.refs_4_), channel_id=1, source_target_pairs={{0,16},{4,20},{8,24},{16,0},{20,4},{24,8},{1,17},{5,21},{9,25},{17... | collective-permute-start | bytes 1179656 | tf_op jit(solution)/shard_map/ppermute | solution.py:689
  62.0 15.4 %collective-permute-start.3 = (bf16[64,3072]{1,0:T(8,128)(2,1)S(1)}, bf16[64,3072]{1,0:T(8,128)(2,1)S(1)}, u32[]{:S(2)}, u32[]{:S(2)}) collective-permute-start(bf16[64,3072]{1,0:T(8,128)(2,1)S(1)} %select_select_fusion), channel_id=1, source_target_pairs={{1,3},{5,7},{9,11},{13,15},{17,19},{21,23},{25,27},{29,31}} | collective-permute-start | bytes 1179656 | tf_op jit(solution)/shard_map/ppermute | solution.py:682
  71.1 13.1 %collective-permute-start.12 = (bf16[12,64,256]{2,1,0:T(8,128)(2,1)S(1)}, bf16[12,64,256]{2,1,0:T(8,128)(2,1)S(1)}, u32[]{:S(2)}, u32[]{:S(2)}) collective-permute-start(bf16[12,64,256]{2,1,0:T(8,128)(2,1)S(1)} %collective-permute-done.11.refs_0_), channel_id=1, source_target_pairs={{0,16},{12,28},{16,0},{28,12},{1,17},{13,29},{17,1},{29,13},{2,18}... | collective-permute-start | bytes 1179656 | tf_op jit(solution)/shard_map/ppermute | solution.py:689
  88.2 2.8 %collective-permute-start.21 = (bf16[64,6144]{1,0:T(8,128)(2,1)S(1)}, bf16[64,6144]{1,0:T(8,128)(2,1)S(1)}, u32[]{:S(2)}, u32[]{:S(2)}) collective-permute-start(bf16[64,6144]{1,0:T(8,128)(2,1)S(1)} %get-tuple-element.67), channel_id=1, source_target_pairs={{2,1},{6,5},{10,9},{14,13},{18,17},{22,21},{26,25},{30,29}} | collective-permute-start | bytes 2359304 | tf_op jit(solution)/shard_map/ppermute | solution.py:737
  90.3 3.4 %collective-permute-start.23 = (bf16[64,6144]{1,0:T(8,128)(2,1)S(1)}, bf16[64,6144]{1,0:T(8,128)(2,1)S(1)}, u32[]{:S(2)}, u32[]{:S(2)}) collective-permute-start(bf16[64,6144]{1,0:T(8,128)(2,1)S(1)} %get-tuple-element.72), channel_id=1, source_target_pairs={{2,1},{6,5},{10,9},{14,13},{18,17},{22,21},{26,25},{30,29}} | collective-permute-start | bytes 2359304 | tf_op jit(solution)/shard_map/ppermute | solution.py:737
  91.7 17.6 %collective-permute-start.22 = (bf16[64,6144]{1,0:T(8,128)(2,1)S(1)}, bf16[64,6144]{1,0:T(8,128)(2,1)S(1)}, u32[]{:S(2)}, u32[]{:S(2)}) collective-permute-start(bf16[64,6144]{1,0:T(8,128)(2,1)S(1)} %get-tuple-element.77), channel_id=1, source_target_pairs={{1,0},{5,4},{9,8},{13,12},{17,16},{21,20},{25,24},{29,28}} | collective-permute-start | bytes 2359304 | tf_op jit(solution)/shard_map/ppermute | solution.py:737
  93.0 20.3 %collective-permute-start.25 = (bf16[64,6144]{1,0:T(8,128)(2,1)S(1)}, bf16[64,6144]{1,0:T(8,128)(2,1)S(1)}, u32[]{:S(2)}, u32[]{:S(2)}) collective-permute-start(bf16[64,6144]{1,0:T(8,128)(2,1)S(1)} %get-tuple-element.77), channel_id=1, source_target_pairs={{2,1},{6,5},{10,9},{14,13},{18,17},{22,21},{26,25},{30,29}} | collective-permute-start | bytes 2359304 | tf_op jit(solution)/shard_map/ppermute | solution.py:737
  112.1 5.9 %collective-permute-start.24 = (bf16[64,6144]{1,0:T(8,128)(2,1)S(1)}, bf16[64,6144]{1,0:T(8,128)(2,1)S(1)}, u32[]{:S(2)}, u32[]{:S(2)}) collective-permute-start(bf16[64,6144]{1,0:T(8,128)(2,1)S(1)} %get-tuple-element.82), channel_id=1, source_target_pairs={{1,0},{5,4},{9,8},{13,12},{17,16},{21,20},{25,24},{29,28}} | collective-permute-start | bytes 2359304 | tf_op jit(solution)/shard_map/ppermute | solution.py:737
  120.5 6.1 %collective-permute-start.26 = (bf16[64,6144]{1,0:T(8,128)(2,1)S(1)}, bf16[64,6144]{1,0:T(8,128)(2,1)S(1)}, u32[]{:S(2)}, u32[]{:S(2)}) collective-permute-start(bf16[64,6144]{1,0:T(8,128)(2,1)S(1)} %get-tuple-element.86), channel_id=1, source_target_pairs={{1,0},{5,4},{9,8},{13,12},{17,16},{21,20},{25,24},{29,28}} | collective-permute-start | bytes 2359304 | tf_op jit(solution)/shard_map/ppermute | solution.py:737
  135.1 25.9 %collective-permute-start.34 = (bf16[25,64,256]{2,1,0:T(8,128)(2,1)S(1)}, bf16[25,64,256]{2,1,0:T(8,128)(2,1)S(1)}, u32[]{:S(2)}, u32[]{:S(2)}) collective-permute-start(bf16[25,64,256]{2,1,0:T(8,128)(2,1)S(1)} %get-tuple-element.98), channel_id=1, source_target_pairs={{0,4},{12,8},{1,5},{13,9},{2,6},{14,10},{3,7},{15,11},{16,20},{28,... | collective-permute-start | bytes 2457608 | tf_op jit(solution)/shard_map/ppermute | solution.py:685
  142.4 27.0 %collective-permute-start.29 = (bf16[64,3072]{1,0:T(8,128)(2,1)S(1)}, bf16[64,3072]{1,0:T(8,128)(2,1)S(1)}, u32[]{:S(2)}, u32[]{:S(2)}) collective-permute-start(bf16[64,3072]{1,0:T(8,128)(2,1)S(1)} %get-tuple-element.91.refs_0_), channel_id=1, source_target_pairs={{0,8},{4,12},{8,0},{12,4},{1,9},{5,13},{9,1},{13,5},{2,10},{6,14},... | collective-permute-start | bytes 1179656 | tf_op jit(solution)/shard_map/ppermute | solution.py:685
  142.5 35.4 %collective-permute-start.27 = (bf16[64,3072]{1,0:T(8,128)(2,1)S(1)}, bf16[64,3072]{1,0:T(8,128)(2,1)S(1)}, u32[]{:S(2)}, u32[]{:S(2)}) collective-permute-start(bf16[64,3072]{1,0:T(8,128)(2,1)S(1)} %get-tuple-element.91.refs_0_), channel_id=1, source_target_pairs={{0,4},{4,8},{8,12},{1,5},{5,9},{9,13},{2,6},{6,10},{10,14},{3,7},{... | collective-permute-start | bytes 1179656 | tf_op jit(solution)/shard_map/ppermute | solution.py:685
  145.2 87.8 %collective-permute-start.31 = (bf16[25,64,256]{2,1,0:T(8,128)(2,1)S(1)}, bf16[25,64,256]{2,1,0:T(8,128)(2,1)S(1)}, u32[]{:S(2)}, u32[]{:S(2)}) collective-permute-start(bf16[25,64,256]{2,1,0:T(8,128)(2,1)S(1)} %get-tuple-element.95), channel_id=1, source_target_pairs={{0,4},{4,8},{8,12},{1,5},{5,9},{9,13},{2,6},{6,10},{10,14},{3,7},{... | collective-permute-start | bytes 2457608 | tf_op jit(solution)/shard_map/ppermute | solution.py:685
  149.9 83.1 %collective-permute-start.32 = (bf16[25,64,256]{2,1,0:T(8,128)(2,1)S(1)}, bf16[25,64,256]{2,1,0:T(8,128)(2,1)S(1)}, u32[]{:S(2)}, u32[]{:S(2)}) collective-permute-start(bf16[25,64,256]{2,1,0:T(8,128)(2,1)S(1)} %get-tuple-element.96), channel_id=1, source_target_pairs={{4,0},{8,4},{12,8},{5,1},{9,5},{13,9},{6,2},{10,6},{14,10},{7,3},{... | collective-permute-start | bytes 2457608 | tf_op jit(solution)/shard_map/ppermute | solution.py:685
  161.0 72.0 %collective-permute-start.33 = (bf16[25,64,256]{2,1,0:T(8,128)(2,1)S(1)}, bf16[25,64,256]{2,1,0:T(8,128)(2,1)S(1)}, u32[]{:S(2)}, u32[]{:S(2)}) collective-permute-start(bf16[25,64,256]{2,1,0:T(8,128)(2,1)S(1)} %get-tuple-element.97), channel_id=1, source_target_pairs={{0,8},{12,4},{1,9},{13,5},{2,10},{14,6},{3,11},{15,7},{16,24},{28,... | collective-permute-start | bytes 2457608 | tf_op jit(solution)/shard_map/ppermute | solution.py:685
  169.5 63.6 %collective-permute-start.35 = (bf16[25,64,256]{2,1,0:T(8,128)(2,1)S(1)}, bf16[25,64,256]{2,1,0:T(8,128)(2,1)S(1)}, u32[]{:S(2)}, u32[]{:S(2)}) collective-permute-start(bf16[25,64,256]{2,1,0:T(8,128)(2,1)S(1)} %add_convert_fusion), channel_id=1, source_target_pairs={{4,12},{8,0},{5,13},{9,1},{6,14},{10,2},{7,15},{11,3},{20,28},{24,... | collective-permute-start | bytes 2457608 | tf_op jit(solution)/shard_map/ppermute | solution.py:685
  177.9 14.2 %collective-permute-start.28 = (bf16[64,3072]{1,0:T(8,128)(2,1)S(1)}, bf16[64,3072]{1,0:T(8,128)(2,1)S(1)}, u32[]{:S(2)}, u32[]{:S(2)}) collective-permute-start(bf16[64,3072]{1,0:T(8,128)(2,1)S(1)} %get-tuple-element.91.refs_0_), channel_id=1, source_target_pairs={{4,0},{8,4},{12,8},{5,1},{9,5},{13,9},{6,2},{10,6},{14,10},{7,3},{... | collective-permute-start | bytes 1179656 | tf_op jit(solution)/shard_map/ppermute | solution.py:685
  192.1 38.8 %collective-permute-start.30 = (bf16[64,3072]{1,0:T(8,128)(2,1)S(1)}, bf16[64,3072]{1,0:T(8,128)(2,1)S(1)}, u32[]{:S(2)}, u32[]{:S(2)}) collective-permute-start(bf16[64,3072]{1,0:T(8,128)(2,1)S(1)} %collective-permute-done.29.refs_3_), channel_id=1, source_target_pairs={{4,0},{8,12},{5,1},{9,13},{6,2},{10,14},{7,3},{11,15},{20,16},{24,... | collective-permute-start | bytes 1179656 | tf_op jit(solution)/shard_map/ppermute | solution.py:685
  (21 other events, 386.6 us)

commit v2 on v1

--- a/solution.py
+++ b/solution.py
@@ -494,11 +494,24 @@
     block = half + 2 * rank
     copies = []
 
-    def send(source, goal):
-        copies.append(pltpu.make_async_copy(source, goal, sem.at[len(copies)]))
-        copies[-1].start()
-
-    spots = [meta_ref[0, field] for field in fields]
+    def send(number, source, goal):
+        copies.append((number, pltpu.make_async_copy(source, goal, sem.at[len(copies)])))
+
+        @pl.when(wanted[number])
+        def _():
+            copies[-1][1].start()
+
+    spots = [meta_ref[0, place] for place, _ in fields]
+    wanted = [meta_ref[0, valid] == 1 for _, valid in fields]
+    gain_s[...] = jnp.zeros_like(gain_s)
+    for number, (out, spot) in enumerate(zip(outs, spots)):
+        size = half // parts
+        for row, low in enumerate(range(0, size, rank)):
+            high = min(low + rank, size)
+            start = pl.multiple_of(spot * size + low, 128)
+            gain = jnp.sum(sums_ref[:, :, pl.ds(start, high - low)], axis=0)
+            gain_s[number, 0, 8 * row : 8 * row + 8, 0 : high - low] = gain.astype(BF16)
+        send(number, gain_s.at[number], out.at[pl.ds(4 * spans, 1)])
     for index in (1, 0):
         base = block * index
         scaled = saved_ref[:, base : base + half]
@@ -507,29 +520,39 @@
         cot = saved_ref[:, 2 * block : 2 * block + half] if index == 1 else first_ref[:, :half]
         for c in range(spans):
             up_s[index, c] = dot_tn(hidden, cot[:, c * rank : (c + 1) * rank]).astype(BF16)
-        for out, spot in zip(outs, spots):
+        for number, (out, spot) in enumerate(zip(outs, spots)):
             start = pl.multiple_of(spot * part, part)
             send(
+                number,
                 up_s.at[index, :, pl.ds(start, part)],
                 out.at[pl.ds((2 * index + 1) * spans, spans)],
             )
-        down_s[index] = dot_tn(scaled, grad_pre).astype(BF16).reshape(down_s.shape[1:])
-        for out, spot in zip(outs, spots):
+        turned = dot_tn(grad_pre, scaled).astype(BF16)
+        size = half // parts
+        each, rest = rank // part, size % rank
+        for p in range(parts):
+            first, entry = p * size, p * spans
+            for low in range(first, first + size - rest, rank):
+                square = turned[:, low : low + rank].reshape(each, part, rank)
+                down_s[index, entry : entry + each] = square
+                entry += each
+            for group in range(rank // rest if rest else 0):
+                low = first + size - rest
+                piece = turned[group * rest : (group + 1) * rest, low : low + rest]
+                down_s[
+                    index, entry : entry + rest // part, :, group * rest : (group + 1) * rest
+                ] = piece.reshape(rest // part, part, rest)
+        for number, (out, spot) in enumerate(zip(outs, spots)):
             send(
+                number,
                 down_s.at[index, pl.ds(spot * spans, spans)],
                 out.at[pl.ds(2 * index * spans, spans)],
             )
-    gain_s[...] = jnp.zeros_like(gain_s)
-    for number, (out, spot) in enumerate(zip(outs, spots)):
-        size = half // parts
-        for row, low in enumerate(range(0, size, rank)):
-            high = min(low + rank, size)
-            start = pl.multiple_of(spot * size + low, 128)
-            gain = jnp.sum(sums_ref[:, :, pl.ds(start, high - low)], axis=0)
-            gain_s[number, 0, 8 * row : 8 * row + 8, 0 : high - low] = gain.astype(BF16)
-        send(gain_s.at[number], out.at[pl.ds(4 * spans, 1)])
-    for copy in copies:
-        copy.wait()
+    for number, copy in copies:
+
+        @pl.when(wanted[number])
+        def _():
+            copy.wait()
 
 
 def weight_call(meta, saved, pairs, sums, fields, parts, half, rank):
@@ -567,7 +590,18 @@
 
     for index in range(2):
         base = 2 * index * spans
-        down_ref[index] = total(slice(base, base + spans))
+        part = messages[0].shape[1]
+        size = spans * part
+        each, rest = rank // part, size % rank
+        for entry in range(0, (size - rest) // part, each):
+            square = total(slice(base + entry, base + entry + each)).reshape(rank, rank)
+            down_ref[index, entry : entry + each] = square.T.reshape(each, part, rank)
+        if rest:
+            entry = (size - rest) // part
+            block = total(slice(base + entry, base + spans)).reshape(rest, rank)
+            for low in range(0, rank, rest):
+                turned = block[:, low : low + rest].T.reshape(rest // part, part, rest)
+                down_ref[index, entry:, :, low : low + rest] = turned
         for c in range(spans):
             up_ref[index, :, c * rank : (c + 1) * rank] = total(base + spans + c)
     size = gain_ref.shape[1]
@@ -753,7 +787,7 @@
 
     if direct:
         own_w, right_w, left_w, far_w, relay_w = weight_call(
-            meta, saved, pairs, sums, (7, 13, 12, 14, 15), parts, half, rank
+            meta, saved, pairs, sums, ((7, 19), (13, 17), (12, 16), (14, 19), (15, 18)), parts, half, rank
         )
         handed = along(relay_w, [(0, 1), (3, 2)])
         outer = along(far_w, [(0, 2), (3, 1)])
@@ -763,7 +797,7 @@
         messages = [own_w, from_left, from_right, outer, inner]
         down_sum, up_sum, gain_sum = total_call(messages, 1.0 / devices, half)
     else:
-        (whole,) = weight_call(meta, saved, pairs, sums, (7,), parts, half, rank)
+        (whole,) = weight_call(meta, saved, pairs, sums, ((7, 19),), parts, half, rank)
         down_sum, up_sum, gain_sum = total_call([whole], 1.0 / devices, half)
         scatter = functools.partial(lax.psum_scatter, axis_name="dp", scatter_dimension=1, tiled=True)
         down_sum, up_sum, gain_sum = scatter(down_sum), scatter(up_sum), scatter(gain_sum)

time: 235 us -> 234 us (level)
  no operation moved by 1% of the time
where the time goes in v2:
time: 234 us; the launch traced here: 233 us
  waiting for transfers between devices  138 us (59%)
  starting transfers between devices  59.5 us (25%)
  Pallas kernels  27.7 us (12%)
  between operations  3.85 us (2%)
    ppermute x13, waiting for transfers between devices, along(): return lax.ppermute(array, 'dp', pairs)  107 us
    ppermute x13, starting transfers between devices, along(): return lax.ppermute(array, 'dp', pairs)  34.4 us
    ppermute x9, waiting for transfers between devices, device_program(): table[slot] = lax.ppermute(packet, 'section', hops)  24.9 us
    pallas_call x7, Pallas kernels, stage_call(): pl.pallas_call(functools.partial(stage_kernel, slot, held, len(shapes) -...  10.3 us
    ppermute x9, starting transfers between devices, device_program(): table[slot] = lax.ppermute(packet, 'section', hops)  8.14 us
    ppermute x4, starting transfers between devices, across(): return lax.ppermute(array, ('groups', 'dp'), pairs)  8.04 us
    ppermute x4, waiting for transfers between devices, across(): return lax.ppermute(array, ('groups', 'dp'), pairs)  6.13 us
    pallas_call x1, Pallas kernels, weight_call(): pl.pallas_call(functools.partial(weight_kernel, fields), grid_spec=pltpu....  5.08 us
  transfers between devices with their start and end apart: 36, of which 12 were waited for; matrix products, arithmetic and copies ran while one was open for 1% of the time, Pallas kernels for 4%

profile of v2, /device:TPU:0, one launch (start us, length us, event | category | flops | bytes accessed | tf_op | source)
XLA Modules:
  0.0 233.5 jit_solution(9569321910185956784)
XLA Ops:
  2.0 3.4 %pack.1 = (bf16[12,64,256]{2,1,0:T(8,128)(2,1)}, bf16[12,64,256]{2,1,0:T(8,128)(2,1)}, bf16[64,3072]{1,0:T(8,128)(2,1)}, bf16[64,3072]{1,0:T(8,128)(2,1)}, bf16[64,3072]{1,0:T(8,128)(2,1)}) custom-call(s32[7,27]{1,0:T(8,128)} %stack.2.meta_ref.refs_0_, bf16[2,6,64,256]{3,2,1,0:T(8,128)(2,1)} %bitcast.18, bf16[2,64,1536]{2,1,0:T(8,128)(2,1)} %bitcast.19, ...), custom_call_target="tpu_custom_call" | custom-call | tf_op jit(solution)/shard_map/pack/pallas_call | solution.py:205
  5.4 5.8 %collective-permute-start.13 = (bf16[12,64,256]{2,1,0:T(8,128)(2,1)}, bf16[12,64,256]{2,1,0:T(8,128)(2,1)}, u32[]{:S(2)}, u32[]{:S(2)}) collective-permute-start(bf16[12,64,256]{2,1,0:T(8,128)(2,1)} %get-tuple-element.56.refs_0_), channel_id=1, source_target_pairs={{0,4},{4,8},{8,12},{1,5},{5,9},{9,13},{2,6},{6,10},{10,14},{3,7},{... | collective-permute-start | bytes 1179656 | tf_op jit(solution)/shard_map/ppermute | solution.py:719
  17.5 3.0 %collective-permute-start.10 = (bf16[12,64,256]{2,1,0:T(8,128)(2,1)S(1)}, bf16[12,64,256]{2,1,0:T(8,128)(2,1)}, u32[]{:S(2)}, u32[]{:S(2)}) collective-permute-start(bf16[12,64,256]{2,1,0:T(8,128)(2,1)S(1)} %copy-done.3), channel_id=1, source_target_pairs={{0,8},{4,12},{8,0},{12,4},{1,9},{5,13},{9,1},{13,5},{2,10},{6,14},... | collective-permute-start | bytes 1179656 | tf_op jit(solution)/shard_map/ppermute | solution.py:719
  20.5 1.4 collective-permute-start
  22.5 1.4 collective-permute-start.1
  23.9 1.4 collective-permute-start.2
  28.7 2.7 %collective-permute-done.15.refs_4_ = bf16[12,64,256]{2,1,0:T(8,128)(2,1)} collective-permute-done((bf16[12,64,256]{2,1,0:T(8,128)(2,1)S(1)}, bf16[12,64,256]{2,1,0:T(8,128)(2,1)}, u32[]{:S(2)}, u32[]{:S(2)}) %collective-permute-start.15) | collective-permute-done | bytes 393248 | tf_op jit(solution)/shard_map/ppermute | solution.py:719
  32.0 23.7 %collective-permute-done.10.refs_6_ = bf16[12,64,256]{2,1,0:T(8,128)(2,1)} collective-permute-done((bf16[12,64,256]{2,1,0:T(8,128)(2,1)S(1)}, bf16[12,64,256]{2,1,0:T(8,128)(2,1)}, u32[]{:S(2)}, u32[]{:S(2)}) %collective-permute-start.10) | collective-permute-done | bytes 393248 | tf_op jit(solution)/shard_map/ppermute | solution.py:719
  55.8 1.5 collective-permute-start.17
  59.3 2.4 %collective-permute-start.16 = (bf16[12,64,256]{2,1,0:T(8,128)(2,1)}, bf16[12,64,256]{2,1,0:T(8,128)(2,1)S(1)}, u32[]{:S(2)}, u32[]{:S(2)}) collective-permute-start(bf16[12,64,256]{2,1,0:T(8,128)(2,1)} %collective-permute-done.15.refs_4_), channel_id=1, source_target_pairs={{0,16},{4,20},{8,24},{16,0},{20,4},{24,8},{1,17},{5,21},{9,25},{17... | collective-permute-start | bytes 1179656 | tf_op jit(solution)/shard_map/ppermute | solution.py:723
  62.6 8.4 %collective-permute-done.11.refs_0_ = bf16[12,64,256]{2,1,0:T(8,128)(2,1)S(1)} collective-permute-done((bf16[12,64,256]{2,1,0:T(8,128)(2,1)}, bf16[12,64,256]{2,1,0:T(8,128)(2,1)S(1)}, u32[]{:S(2)}, u32[]{:S(2)}) %collective-permute-start.11) | collective-permute-done | bytes 393248 | tf_op jit(solution)/shard_map/ppermute | solution.py:719
  71.1 3.4 %collective-permute-start.12 = (bf16[12,64,256]{2,1,0:T(8,128)(2,1)S(1)}, bf16[12,64,256]{2,1,0:T(8,128)(2,1)S(1)}, u32[]{:S(2)}, u32[]{:S(2)}) collective-permute-start(bf16[12,64,256]{2,1,0:T(8,128)(2,1)S(1)} %collective-permute-done.11.refs_0_), channel_id=1, source_target_pairs={{0,16},{12,28},{16,0},{28,12},{1,17},{13,29},{17,1},{29,13},{2,18}... | collective-permute-start | bytes 1179656 | tf_op jit(solution)/shard_map/ppermute | solution.py:723
  74.6 2.8 %assemble.2 = (bf16[2,24,64,256]{3,2,1,0:T(8,128)(2,1)S(1)}, bf16[2,6,256,256]{3,2,1,0:T(8,128)(2,1)S(1)}) custom-call(s32[7,27]{1,0:T(8,128)S(1)} %copy-done.1, bf16[12,64,256]{2,1,0:T(8,128)(2,1)S(1)} %copy-done.3, bf16[12,64,256]{2,1,0:T(8,128)(2,1)S(1)} %copy-done.4, bf16[12,64,256]{2,1,0:T(8,128)(2,1)} %collective-permute-done.13.refs_2_, ...), custom_call_target="tpu_custom_call" | custom-call | tf_op jit(solution)/shard_map/assemble/pallas_call | solution.py:258
  78.1 6.1 %collective-permute-done.12.refs_1_ = bf16[12,64,256]{2,1,0:T(8,128)(2,1)S(1)} collective-permute-done((bf16[12,64,256]{2,1,0:T(8,128)(2,1)S(1)}, bf16[12,64,256]{2,1,0:T(8,128)(2,1)S(1)}, u32[]{:S(2)}, u32[]{:S(2)}) %collective-permute-start.12) | collective-permute-done | bytes 393248 | tf_op jit(solution)/shard_map/ppermute | solution.py:723
  93.7 15.6 %collective-permute-done.22.refs_5_ = bf16[64,6144]{1,0:T(8,128)(2,1)S(1)} collective-permute-done((bf16[64,6144]{1,0:T(8,128)(2,1)S(1)}, bf16[64,6144]{1,0:T(8,128)(2,1)S(1)}, u32[]{:S(2)}, u32[]{:S(2)}) %collective-permute-start.22) | collective-permute-done | bytes 786464 | tf_op jit(solution)/shard_map/ppermute | solution.py:771
  109.3 2.7 %stage.11 = (bf16[64,6144]{1,0:T(8,128)(2,1)S(1)}, bf16[192,3072]{1,0:T(8,128)(2,1)S(1)}, bf16[192,5632]{1,0:T(8,128)(2,1)S(1)}, f32[3,8,1536]{2,1,0:T(8,128)S(1)}, bf16[64,3072]{1,0:T(8,128)(2,1)S(1)}) custom-call(s32[7,27]{1,0:T(8,128)S(1)} %copy-done.1, ...), custom_call_target="tpu_custom_call", output_to_operand_aliasing={{1}: (7, {}), {2}: (8, {}), {3}: (9, {}), {4}: (10, {})} | custom-call | flops 805306368 | bytes 1572864 | tf_op jit(solution)/shard_map/stage/pallas_call | solution.py:465
  113.4 4.6 %collective-permute-done.24.refs_5_ = bf16[64,6144]{1,0:T(8,128)(2,1)S(1)} collective-permute-done((bf16[64,6144]{1,0:T(8,128)(2,1)S(1)}, bf16[64,6144]{1,0:T(8,128)(2,1)S(1)}, u32[]{:S(2)}, u32[]{:S(2)}) %collective-permute-start.24) | collective-permute-done | bytes 786464 | tf_op jit(solution)/shard_map/ppermute | solution.py:771
  117.9 2.5 %stage.12 = (bf16[64,6144]{1,0:T(8,128)(2,1)S(1)}, bf16[192,3072]{1,0:T(8,128)(2,1)S(1)}, bf16[192,5632]{1,0:T(8,128)(2,1)S(1)}, f32[3,8,1536]{2,1,0:T(8,128)S(1)}) custom-call(s32[7,27]{1,0:T(8,128)S(1)} %copy-done.1, bf16[2,1536]{1,0:T(2,128)(2,1)S(1)} %bitcast.13, ...), custom_call_target="tpu_custom_call", output_to_operand_aliasing={{1}: (7, {}), {2}: (8, {}), {3}: (9, {})} | custom-call | flops 805306368 | bytes 1572864 | tf_op jit(solution)/shard_map/stage/pallas_call | solution.py:465
  121.8 4.8 %collective-permute-done.26.refs_5_ = bf16[64,6144]{1,0:T(8,128)(2,1)S(1)} collective-permute-done((bf16[64,6144]{1,0:T(8,128)(2,1)S(1)}, bf16[64,6144]{1,0:T(8,128)(2,1)S(1)}, u32[]{:S(2)}, u32[]{:S(2)}) %collective-permute-start.26) | collective-permute-done | bytes 786464 | tf_op jit(solution)/shard_map/ppermute | solution.py:771
  126.5 2.5 %stage.13 = (bf16[192,3072]{1,0:T(8,128)(2,1)S(1)}, bf16[192,5632]{1,0:T(8,128)(2,1)S(1)}, f32[3,8,1536]{2,1,0:T(8,128)S(1)}) custom-call(s32[7,27]{1,0:T(8,128)S(1)} %copy-done.1, bf16[2,1536]{1,0:T(2,128)(2,1)S(1)} %bitcast.14, bf16[192,6144]{1,0:T(8,128)(2,1)S(1)} %head.1.refs_2_, ...), custom_call_target="tpu_custom_call", output_to_operand_aliasing={{0}: (6, {}), {1}: (7, {}), {2}: (8, {})} | custom-call | flops 805306368 | bytes 1572864 | tf_op jit(solution)/shard_map/stage/pallas_call | solution.py:465
  129.0 5.1 %weight.1 = (bf16[25,64,256]{2,1,0:T(8,128)(2,1)S(1)}, bf16[25,64,256]{2,1,0:T(8,128)(2,1)S(1)}, bf16[25,64,256]{2,1,0:T(8,128)(2,1)S(1)}, bf16[25,64,256]{2,1,0:T(8,128)(2,1)S(1)}, bf16[25,64,256]{2,1,0:T(8,128)(2,1)S(1)}) custom-call(s32[7,27]{1,0:T(8,128)S(1)} %copy-done.1, bf16[192,5632]{1,0:T(8,128)(2,1)S(1)} %get-tuple-element.92.saved_ref, ...), custom_call_target="tpu_custom_call" | custom-call | tf_op jit(solution)/shard_map/weight/pallas_call | solution.py:560
  134.1 7.3 %collective-permute-start.34 = (bf16[25,64,256]{2,1,0:T(8,128)(2,1)S(1)}, bf16[25,64,256]{2,1,0:T(8,128)(2,1)S(1)}, u32[]{:S(2)}, u32[]{:S(2)}) collective-permute-start(bf16[25,64,256]{2,1,0:T(8,128)(2,1)S(1)} %get-tuple-element.98), channel_id=1, source_target_pairs={{0,4},{12,8},{1,5},{13,9},{2,6},{14,10},{3,7},{15,11},{16,20},{28,... | collective-permute-start | bytes 2457608 | tf_op jit(solution)/shard_map/ppermute | solution.py:719
  141.5 2.7 %collective-permute-start.27 = (bf16[64,3072]{1,0:T(8,128)(2,1)S(1)}, bf16[64,3072]{1,0:T(8,128)(2,1)S(1)}, u32[]{:S(2)}, u32[]{:S(2)}) collective-permute-start(bf16[64,3072]{1,0:T(8,128)(2,1)S(1)} %get-tuple-element.91.refs_0_), channel_id=1, source_target_pairs={{0,4},{4,8},{8,12},{1,5},{5,9},{9,13},{2,6},{6,10},{10,14},{3,7},{... | collective-permute-start | bytes 1179656 | tf_op jit(solution)/shard_map/ppermute | solution.py:719
  144.2 4.6 %collective-permute-start.31 = (bf16[25,64,256]{2,1,0:T(8,128)(2,1)S(1)}, bf16[25,64,256]{2,1,0:T(8,128)(2,1)S(1)}, u32[]{:S(2)}, u32[]{:S(2)}) collective-permute-start(bf16[25,64,256]{2,1,0:T(8,128)(2,1)S(1)} %get-tuple-element.95), channel_id=1, source_target_pairs={{0,4},{4,8},{8,12},{1,5},{5,9},{9,13},{2,6},{6,10},{10,14},{3,7},{... | collective-permute-start | bytes 2457608 | tf_op jit(solution)/shard_map/ppermute | solution.py:719
  150.1 9.8 %collective-permute-done.34 = bf16[25,64,256]{2,1,0:T(8,128)(2,1)S(1)} collective-permute-done((bf16[25,64,256]{2,1,0:T(8,128)(2,1)S(1)}, bf16[25,64,256]{2,1,0:T(8,128)(2,1)S(1)}, u32[]{:S(2)}, u32[]{:S(2)}) %collective-permute-start.34) | collective-permute-done | bytes 819232 | tf_op jit(solution)/shard_map/ppermute | solution.py:719
  160.0 3.2 %collective-permute-start.33 = (bf16[25,64,256]{2,1,0:T(8,128)(2,1)S(1)}, bf16[25,64,256]{2,1,0:T(8,128)(2,1)S(1)}, u32[]{:S(2)}, u32[]{:S(2)}) collective-permute-start(bf16[25,64,256]{2,1,0:T(8,128)(2,1)S(1)} %get-tuple-element.97), channel_id=1, source_target_pairs={{0,8},{12,4},{1,9},{13,5},{2,10},{14,6},{3,11},{15,7},{16,24},{28,... | collective-permute-start | bytes 2457608 | tf_op jit(solution)/shard_map/ppermute | solution.py:719
  163.5 5.0 %collective-permute-done.29.refs_3_ = bf16[64,3072]{1,0:T(8,128)(2,1)S(1)} collective-permute-done((bf16[64,3072]{1,0:T(8,128)(2,1)S(1)}, bf16[64,3072]{1,0:T(8,128)(2,1)S(1)}, u32[]{:S(2)}, u32[]{:S(2)}) %collective-permute-start.29) | collective-permute-done | bytes 393248 | tf_op jit(solution)/shard_map/ppermute | solution.py:719
  169.7 7.1 %collective-permute-done.27.refs_1_ = bf16[64,3072]{1,0:T(8,128)(2,1)S(1)} collective-permute-done((bf16[64,3072]{1,0:T(8,128)(2,1)S(1)}, bf16[64,3072]{1,0:T(8,128)(2,1)S(1)}, u32[]{:S(2)}, u32[]{:S(2)}) %collective-permute-start.27) | collective-permute-done | bytes 393248 | tf_op jit(solution)/shard_map/ppermute | solution.py:719
  178.2 12.9 %collective-permute-done.28.refs_2_ = bf16[64,3072]{1,0:T(8,128)(2,1)S(1)} collective-permute-done((bf16[64,3072]{1,0:T(8,128)(2,1)S(1)}, bf16[64,3072]{1,0:T(8,128)(2,1)S(1)}, u32[]{:S(2)}, u32[]{:S(2)}) %collective-permute-start.28) | collective-permute-done | bytes 393248 | tf_op jit(solution)/shard_map/ppermute | solution.py:719
  192.4 37.5 %collective-permute-done.30.refs_4_ = bf16[64,3072]{1,0:T(8,128)(2,1)S(1)} collective-permute-done((bf16[64,3072]{1,0:T(8,128)(2,1)S(1)}, bf16[64,3072]{1,0:T(8,128)(2,1)S(1)}, u32[]{:S(2)}, u32[]{:S(2)}) %collective-permute-start.30) | collective-permute-done | bytes 393248 | tf_op jit(solution)/shard_map/ppermute | solution.py:719
  229.9 2.0 output.1
  232.0 1.5 total.1
  (121 shorter events, 30.5 us)
Async XLA Ops:
  5.4 18.5 %collective-permute-start.13 = (bf16[12,64,256]{2,1,0:T(8,128)(2,1)}, bf16[12,64,256]{2,1,0:T(8,128)(2,1)}, u32[]{:S(2)}, u32[]{:S(2)}) collective-permute-start(bf16[12,64,256]{2,1,0:T(8,128)(2,1)} %get-tuple-element.56.refs_0_), channel_id=1, source_target_pairs={{0,4},{4,8},{8,12},{1,5},{5,9},{9,13},{2,6},{6,10},{10,14},{3,7},{... | collective-permute-start | bytes 1179656 | tf_op jit(solution)/shard_map/ppermute | solution.py:719
  11.3 2.7 %collective-permute-start.4 = (bf16[768,128]{1,0:T(8,128)(2,1)S(1)}, bf16[768,128]{1,0:T(8,128)(2,1)S(1)}, u32[]{:S(2)}, u32[]{:S(2)}) collective-permute-start(bf16[768,128]{1,0:T(8,128)(2,1)S(1)} %copy-done.2), channel_id=1, source_target_pairs={{3,7},{7,11},{11,15},{15,3},{19,23},{23,27},{27,31},{31,19}} | collective-permute-start | bytes 589832 | tf_op jit(solution)/shard_map/ppermute | solution.py:715
  12.0 2.1 collective-permute-start.5
  14.8 5.7 %collective-permute-start.7 = (f32[8,128]{1,0:T(8,128)S(1)}, f32[8,128]{1,0:T(8,128)S(1)}, u32[]{:S(2)}, u32[]{:S(2)}) collective-permute-start(f32[8,128]{1,0:T(8,128)S(1)} %score.1.own_ref), channel_id=1, source_target_pairs={{3,15},{7,3},{11,7},{15,11},{19,31},{23,19},{27,23},{31,27}} | collective-permute-start | bytes 12296 | tf_op jit(solution)/shard_map/ppermute | solution.py:744
  15.5 6.4 %collective-permute-start.8 = (f32[8,128]{1,0:T(8,128)S(1)}, f32[8,128]{1,0:T(8,128)S(1)}, u32[]{:S(2)}, u32[]{:S(2)}) collective-permute-start(f32[8,128]{1,0:T(8,128)S(1)} %score.1.own_ref), channel_id=1, source_target_pairs={{3,11},{7,15},{11,3},{15,7},{19,27},{23,31},{27,19},{31,23}} | collective-permute-start | bytes 12296 | tf_op jit(solution)/shard_map/ppermute | solution.py:744
  16.2 15.2 %collective-permute-start.15 = (bf16[12,64,256]{2,1,0:T(8,128)(2,1)S(1)}, bf16[12,64,256]{2,1,0:T(8,128)(2,1)}, u32[]{:S(2)}, u32[]{:S(2)}) collective-permute-start(bf16[12,64,256]{2,1,0:T(8,128)(2,1)S(1)} %copy-done.3), channel_id=1, source_target_pairs={{4,0},{8,4},{12,8},{5,1},{9,5},{13,9},{6,2},{10,6},{14,10},{7,3},{... | collective-permute-start | bytes 1179656 | tf_op jit(solution)/shard_map/ppermute | solution.py:719
  17.5 38.2 %collective-permute-start.10 = (bf16[12,64,256]{2,1,0:T(8,128)(2,1)S(1)}, bf16[12,64,256]{2,1,0:T(8,128)(2,1)}, u32[]{:S(2)}, u32[]{:S(2)}) collective-permute-start(bf16[12,64,256]{2,1,0:T(8,128)(2,1)S(1)} %copy-done.3), channel_id=1, source_target_pairs={{0,8},{4,12},{8,0},{12,4},{1,9},{5,13},{9,1},{13,5},{2,10},{6,14},... | collective-permute-start | bytes 1179656 | tf_op jit(solution)/shard_map/ppermute | solution.py:719
  20.5 36.8 %collective-permute-start = (bf16[64,3072]{1,0:T(8,128)(2,1)}, bf16[64,3072]{1,0:T(8,128)(2,1)}, u32[]{:S(2)}, u32[]{:S(2)}) collective-permute-start(bf16[64,3072]{1,0:T(8,128)(2,1)} %get-tuple-element.53), channel_id=1, source_target_pairs={{1,13},{5,1},{9,5},{13,9},{17,29},{21,17},{25,21},{29,25}} | collective-permute-start | bytes 1179656 | tf_op jit(solution)/shard_map/ppermute | solution.py:710
  22.5 36.0 %collective-permute-start.1 = (bf16[64,3072]{1,0:T(8,128)(2,1)}, bf16[64,3072]{1,0:T(8,128)(2,1)}, u32[]{:S(2)}, u32[]{:S(2)}) collective-permute-start(bf16[64,3072]{1,0:T(8,128)(2,1)} %get-tuple-element.54), channel_id=1, source_target_pairs={{1,9},{5,13},{9,1},{13,5},{17,25},{21,29},{25,17},{29,21}} | collective-permute-start | bytes 1179656 | tf_op jit(solution)/shard_map/ppermute | solution.py:710
  23.9 35.3 %collective-permute-start.2 = (bf16[64,3072]{1,0:T(8,128)(2,1)}, bf16[64,3072]{1,0:T(8,128)(2,1)}, u32[]{:S(2)}, u32[]{:S(2)}) collective-permute-start(bf16[64,3072]{1,0:T(8,128)(2,1)} %get-tuple-element.55), channel_id=1, source_target_pairs={{1,5},{5,9},{9,13},{13,1},{17,21},{21,25},{25,29},{29,17}} | collective-permute-start | bytes 1179656 | tf_op jit(solution)/shard_map/ppermute | solution.py:710
  31.4 30.6 %collective-permute-start.9 = (f32[8,128]{1,0:T(8,128)}, f32[8,128]{1,0:T(8,128)S(1)}, u32[]{:S(2)}, u32[]{:S(2)}) collective-permute-start(f32[8,128]{1,0:T(8,128)} %copy-done.6), channel_id=1, source_target_pairs={{3,7},{7,11},{11,15},{15,3},{19,23},{23,27},{27,31},{31,19}} | collective-permute-start | bytes 12296 | tf_op jit(solution)/shard_map/ppermute | solution.py:744
  55.8 18.8 %collective-permute-start.17 = (bf16[12,64,256]{2,1,0:T(8,128)(2,1)}, bf16[12,64,256]{2,1,0:T(8,128)(2,1)S(1)}, u32[]{:S(2)}, u32[]{:S(2)}) collective-permute-start(bf16[12,64,256]{2,1,0:T(8,128)(2,1)} %collective-permute-done.10.refs_6_), channel_id=1, source_target_pairs={{0,16},{4,20},{8,24},{12,28},{16,0},{20,4},{24,8},{28,12},{1,17},{... | collective-permute-start | bytes 1179656 | tf_op jit(solution)/shard_map/ppermute | solution.py:723
  57.3 13.8 %collective-permute-start.11 = (bf16[12,64,256]{2,1,0:T(8,128)(2,1)}, bf16[12,64,256]{2,1,0:T(8,128)(2,1)S(1)}, u32[]{:S(2)}, u32[]{:S(2)}) collective-permute-start(bf16[12,64,256]{2,1,0:T(8,128)(2,1)} %collective-permute-done.10.refs_6_), channel_id=1, source_target_pairs={{4,0},{8,12},{5,1},{9,13},{6,2},{10,14},{7,3},{11,15},{20,16},{24,... | collective-permute-start | bytes 1179656 | tf_op jit(solution)/shard_map/ppermute | solution.py:719
  58.6 16.0 %collective-permute-start.14 = (bf16[12,64,256]{2,1,0:T(8,128)(2,1)}, bf16[12,64,256]{2,1,0:T(8,128)(2,1)S(1)}, u32[]{:S(2)}, u32[]{:S(2)}) collective-permute-start(bf16[12,64,256]{2,1,0:T(8,128)(2,1)} %collective-permute-done.13.refs_2_), channel_id=1, source_target_pairs={{4,20},{8,24},{12,28},{20,4},{24,8},{28,12},{5,21},{9,25},{13,29},... | collective-permute-start | bytes 1179656 | tf_op jit(solution)/shard_map/ppermute | solution.py:723
  59.3 15.3 %collective-permute-start.16 = (bf16[12,64,256]{2,1,0:T(8,128)(2,1)}, bf16[12,64,256]{2,1,0:T(8,128)(2,1)S(1)}, u32[]{:S(2)}, u32[]{:S(2)}) collective-permute-start(bf16[12,64,256]{2,1,0:T(8,128)(2,1)} %collective-permute-done.15.refs_4_), channel_id=1, source_target_pairs={{0,16},{4,20},{8,24},{16,0},{20,4},{24,8},{1,17},{5,21},{9,25},{17... | collective-permute-start | bytes 1179656 | tf_op jit(solution)/shard_map/ppermute | solution.py:723
  62.0 15.4 %collective-permute-start.3 = (bf16[64,3072]{1,0:T(8,128)(2,1)S(1)}, bf16[64,3072]{1,0:T(8,128)(2,1)S(1)}, u32[]{:S(2)}, u32[]{:S(2)}) collective-permute-start(bf16[64,3072]{1,0:T(8,128)(2,1)S(1)} %select_select_fusion), channel_id=1, source_target_pairs={{1,3},{5,7},{9,11},{13,15},{17,19},{21,23},{25,27},{29,31}} | collective-permute-start | bytes 1179656 | tf_op jit(solution)/shard_map/ppermute | solution.py:716
  71.1 13.1 %collective-permute-start.12 = (bf16[12,64,256]{2,1,0:T(8,128)(2,1)S(1)}, bf16[12,64,256]{2,1,0:T(8,128)(2,1)S(1)}, u32[]{:S(2)}, u32[]{:S(2)}) collective-permute-start(bf16[12,64,256]{2,1,0:T(8,128)(2,1)S(1)} %collective-permute-done.11.refs_0_), channel_id=1, source_target_pairs={{0,16},{12,28},{16,0},{28,12},{1,17},{13,29},{17,1},{29,13},{2,18}... | collective-permute-start | bytes 1179656 | tf_op jit(solution)/shard_map/ppermute | solution.py:723
  88.2 2.8 %collective-permute-start.21 = (bf16[64,6144]{1,0:T(8,128)(2,1)S(1)}, bf16[64,6144]{1,0:T(8,128)(2,1)S(1)}, u32[]{:S(2)}, u32[]{:S(2)}) collective-permute-start(bf16[64,6144]{1,0:T(8,128)(2,1)S(1)} %get-tuple-element.67), channel_id=1, source_target_pairs={{2,1},{6,5},{10,9},{14,13},{18,17},{22,21},{26,25},{30,29}} | collective-permute-start | bytes 2359304 | tf_op jit(solution)/shard_map/ppermute | solution.py:771
  90.3 3.4 %collective-permute-start.23 = (bf16[64,6144]{1,0:T(8,128)(2,1)S(1)}, bf16[64,6144]{1,0:T(8,128)(2,1)S(1)}, u32[]{:S(2)}, u32[]{:S(2)}) collective-permute-start(bf16[64,6144]{1,0:T(8,128)(2,1)S(1)} %get-tuple-element.72), channel_id=1, source_target_pairs={{2,1},{6,5},{10,9},{14,13},{18,17},{22,21},{26,25},{30,29}} | collective-permute-start | bytes 2359304 | tf_op jit(solution)/shard_map/ppermute | solution.py:771
  91.7 17.6 %collective-permute-start.22 = (bf16[64,6144]{1,0:T(8,128)(2,1)S(1)}, bf16[64,6144]{1,0:T(8,128)(2,1)S(1)}, u32[]{:S(2)}, u32[]{:S(2)}) collective-permute-start(bf16[64,6144]{1,0:T(8,128)(2,1)S(1)} %get-tuple-element.77), channel_id=1, source_target_pairs={{1,0},{5,4},{9,8},{13,12},{17,16},{21,20},{25,24},{29,28}} | collective-permute-start | bytes 2359304 | tf_op jit(solution)/shard_map/ppermute | solution.py:771
  93.0 20.3 %collective-permute-start.25 = (bf16[64,6144]{1,0:T(8,128)(2,1)S(1)}, bf16[64,6144]{1,0:T(8,128)(2,1)S(1)}, u32[]{:S(2)}, u32[]{:S(2)}) collective-permute-start(bf16[64,6144]{1,0:T(8,128)(2,1)S(1)} %get-tuple-element.77), channel_id=1, source_target_pairs={{2,1},{6,5},{10,9},{14,13},{18,17},{22,21},{26,25},{30,29}} | collective-permute-start | bytes 2359304 | tf_op jit(solution)/shard_map/ppermute | solution.py:771
  112.1 5.9 %collective-permute-start.24 = (bf16[64,6144]{1,0:T(8,128)(2,1)S(1)}, bf16[64,6144]{1,0:T(8,128)(2,1)S(1)}, u32[]{:S(2)}, u32[]{:S(2)}) collective-permute-start(bf16[64,6144]{1,0:T(8,128)(2,1)S(1)} %get-tuple-element.82), channel_id=1, source_target_pairs={{1,0},{5,4},{9,8},{13,12},{17,16},{21,20},{25,24},{29,28}} | collective-permute-start | bytes 2359304 | tf_op jit(solution)/shard_map/ppermute | solution.py:771
  120.5 6.1 %collective-permute-start.26 = (bf16[64,6144]{1,0:T(8,128)(2,1)S(1)}, bf16[64,6144]{1,0:T(8,128)(2,1)S(1)}, u32[]{:S(2)}, u32[]{:S(2)}) collective-permute-start(bf16[64,6144]{1,0:T(8,128)(2,1)S(1)} %get-tuple-element.86), channel_id=1, source_target_pairs={{1,0},{5,4},{9,8},{13,12},{17,16},{21,20},{25,24},{29,28}} | collective-permute-start | bytes 2359304 | tf_op jit(solution)/shard_map/ppermute | solution.py:771
  134.1 25.9 %collective-permute-start.34 = (bf16[25,64,256]{2,1,0:T(8,128)(2,1)S(1)}, bf16[25,64,256]{2,1,0:T(8,128)(2,1)S(1)}, u32[]{:S(2)}, u32[]{:S(2)}) collective-permute-start(bf16[25,64,256]{2,1,0:T(8,128)(2,1)S(1)} %get-tuple-element.98), channel_id=1, source_target_pairs={{0,4},{12,8},{1,5},{13,9},{2,6},{14,10},{3,7},{15,11},{16,20},{28,... | collective-permute-start | bytes 2457608 | tf_op jit(solution)/shard_map/ppermute | solution.py:719
  141.4 27.0 %collective-permute-start.29 = (bf16[64,3072]{1,0:T(8,128)(2,1)S(1)}, bf16[64,3072]{1,0:T(8,128)(2,1)S(1)}, u32[]{:S(2)}, u32[]{:S(2)}) collective-permute-start(bf16[64,3072]{1,0:T(8,128)(2,1)S(1)} %get-tuple-element.91.refs_0_), channel_id=1, source_target_pairs={{0,8},{4,12},{8,0},{12,4},{1,9},{5,13},{9,1},{13,5},{2,10},{6,14},... | collective-permute-start | bytes 1179656 | tf_op jit(solution)/shard_map/ppermute | solution.py:719
  141.5 35.4 %collective-permute-start.27 = (bf16[64,3072]{1,0:T(8,128)(2,1)S(1)}, bf16[64,3072]{1,0:T(8,128)(2,1)S(1)}, u32[]{:S(2)}, u32[]{:S(2)}) collective-permute-start(bf16[64,3072]{1,0:T(8,128)(2,1)S(1)} %get-tuple-element.91.refs_0_), channel_id=1, source_target_pairs={{0,4},{4,8},{8,12},{1,5},{5,9},{9,13},{2,6},{6,10},{10,14},{3,7},{... | collective-permute-start | bytes 1179656 | tf_op jit(solution)/shard_map/ppermute | solution.py:719
  144.2 87.8 %collective-permute-start.31 = (bf16[25,64,256]{2,1,0:T(8,128)(2,1)S(1)}, bf16[25,64,256]{2,1,0:T(8,128)(2,1)S(1)}, u32[]{:S(2)}, u32[]{:S(2)}) collective-permute-start(bf16[25,64,256]{2,1,0:T(8,128)(2,1)S(1)} %get-tuple-element.95), channel_id=1, source_target_pairs={{0,4},{4,8},{8,12},{1,5},{5,9},{9,13},{2,6},{6,10},{10,14},{3,7},{... | collective-permute-start | bytes 2457608 | tf_op jit(solution)/shard_map/ppermute | solution.py:719
  148.8 83.1 %collective-permute-start.32 = (bf16[25,64,256]{2,1,0:T(8,128)(2,1)S(1)}, bf16[25,64,256]{2,1,0:T(8,128)(2,1)S(1)}, u32[]{:S(2)}, u32[]{:S(2)}) collective-permute-start(bf16[25,64,256]{2,1,0:T(8,128)(2,1)S(1)} %get-tuple-element.96), channel_id=1, source_target_pairs={{4,0},{8,4},{12,8},{5,1},{9,5},{13,9},{6,2},{10,6},{14,10},{7,3},{... | collective-permute-start | bytes 2457608 | tf_op jit(solution)/shard_map/ppermute | solution.py:719
  160.0 72.0 %collective-permute-start.33 = (bf16[25,64,256]{2,1,0:T(8,128)(2,1)S(1)}, bf16[25,64,256]{2,1,0:T(8,128)(2,1)S(1)}, u32[]{:S(2)}, u32[]{:S(2)}) collective-permute-start(bf16[25,64,256]{2,1,0:T(8,128)(2,1)S(1)} %get-tuple-element.97), channel_id=1, source_target_pairs={{0,8},{12,4},{1,9},{13,5},{2,10},{14,6},{3,11},{15,7},{16,24},{28,... | collective-permute-start | bytes 2457608 | tf_op jit(solution)/shard_map/ppermute | solution.py:719
  168.5 63.6 %collective-permute-start.35 = (bf16[25,64,256]{2,1,0:T(8,128)(2,1)S(1)}, bf16[25,64,256]{2,1,0:T(8,128)(2,1)S(1)}, u32[]{:S(2)}, u32[]{:S(2)}) collective-permute-start(bf16[25,64,256]{2,1,0:T(8,128)(2,1)S(1)} %add_convert_fusion), channel_id=1, source_target_pairs={{4,12},{8,0},{5,13},{9,1},{6,14},{10,2},{7,15},{11,3},{20,28},{24,... | collective-permute-start | bytes 2457608 | tf_op jit(solution)/shard_map/ppermute | solution.py:719
  176.9 14.2 %collective-permute-start.28 = (bf16[64,3072]{1,0:T(8,128)(2,1)S(1)}, bf16[64,3072]{1,0:T(8,128)(2,1)S(1)}, u32[]{:S(2)}, u32[]{:S(2)}) collective-permute-start(bf16[64,3072]{1,0:T(8,128)(2,1)S(1)} %get-tuple-element.91.refs_0_), channel_id=1, source_target_pairs={{4,0},{8,4},{12,8},{5,1},{9,5},{13,9},{6,2},{10,6},{14,10},{7,3},{... | collective-permute-start | bytes 1179656 | tf_op jit(solution)/shard_map/ppermute | solution.py:719
  191.1 38.8 %collective-permute-start.30 = (bf16[64,3072]{1,0:T(8,128)(2,1)S(1)}, bf16[64,3072]{1,0:T(8,128)(2,1)S(1)}, u32[]{:S(2)}, u32[]{:S(2)}) collective-permute-start(bf16[64,3072]{1,0:T(8,128)(2,1)S(1)} %collective-permute-done.29.refs_3_), channel_id=1, source_target_pairs={{4,0},{8,12},{5,1},{9,13},{6,2},{10,14},{7,3},{11,15},{20,16},{24,... | collective-permute-start | bytes 1179656 | tf_op jit(solution)/shard_map/ppermute | solution.py:719
  (21 other events, 386.6 us)
